TPU v7x, 32 devices: a whole 2x2x4 slice. The times are simulated.
32 devices in a mesh: blk: 4 (over y, x), uly: 8 (over z, core).
Axes of the slice: x: 2, y: 2, z: 4, core: 2. Of those that a mesh axis runs over, the one named last changes fastest.
Arguments:
- query_proj: bfloat16 [2048, 1024], P(('blk', 'uly')), may hold values from -8 to 8
- key_proj: bfloat16 [2048, 1024], P(('blk', 'uly')), may hold values from -8 to 8
- value_proj: bfloat16 [2048, 1024], P(('blk', 'uly')), may hold values from -6 to 6
- attn_output: bfloat16 [2048, 1024], P(('blk', 'uly')), may hold values from -6 to 6
- out_grad: bfloat16 [2048, 1024], P(('blk', 'uly')), may hold values from -6 to 6
- random_blocks: int32 [16, 3], replicated, may hold values from 0 to 14, as said below
Outputs:
- query_grad: bfloat16 [2048, 1024], P(('blk', 'uly'))
- key_grad: bfloat16 [2048, 1024], P(('blk', 'uly'))
- value_grad: bfloat16 [2048, 1024], P(('blk', 'uly'))
Inputs may be any that keep to these rules, and one draw needn't show every extreme that they name: `random_blocks`: every entry of row i names a block below i; row 0 names only block 0. The rows of one shard of blk (4 rows in a row, aligned) name at most 2 distinct blocks that lie in any one other shard, exactly 2 that lie in the shard just before theirs, and the rows of the last shard name exactly 2 that lie in the first shard.
All inputs are finite; a program needn't handle non-finite values.
Results may differ from a plain program's by a relative error of at most 0.005.
Values may be sent and summed in bfloat16 or wider, within the bound.
A program may use at most 64 MiB of HBM per device.

v0:
```python
import functools
import math

import jax
import jax.numpy as jnp
from jax import lax
from jax.experimental import pallas as pl
from jax.experimental.pallas import tpu as pltpu
from jax.sharding import PartitionSpec as P

HD = 128
BLOCK = 128
RAND = 3
CAP = 2


def named_table(random_blocks, per_shard):
    block_count = random_blocks.shape[0]
    shard_count = block_count // per_shard
    entries = random_blocks.reshape(shard_count, per_shard * RAND)
    block_ids = jnp.arange(block_count, dtype=jnp.int32)
    named = jnp.any(entries[:, :, None] == block_ids[None, None, :], axis=1)
    owner = block_ids // per_shard
    named = named & (owner[None, :] != jnp.arange(shard_count, dtype=jnp.int32)[:, None])
    grouped = named.reshape(shard_count, shard_count, per_shard).astype(jnp.int32)
    rank_in = jnp.cumsum(grouped, axis=2) - grouped
    return (grouped, rank_in)


def send_slots(grouped, rank_in, cycle_rank, per_shard):
    mine = lax.dynamic_index_in_dim(grouped, cycle_rank, 1, keepdims=False)
    mine_rank = lax.dynamic_index_in_dim(rank_in, cycle_rank, 1, keepdims=False)
    slot_ids = jnp.arange(CAP, dtype=jnp.int32)
    hit = (mine[:, None, :] == 1) & (mine_rank[:, None, :] == slot_ids[None, :, None])
    positions = jnp.arange(per_shard, dtype=jnp.int32)
    select = jnp.sum(jnp.where(hit, positions[None, None, :], 0), axis=2)
    filled = jnp.any(hit, axis=2)
    return (select, filled)


def on_device(query_proj, key_proj, value_proj, attn_output, out_grad, random_blocks):
    tok_count = query_proj.shape[0]
    head_count = query_proj.shape[1] // HD
    score_scale = HD ** (-0.5)
    extent = 3 + RAND

    def to_heads(tensor):
        return tensor.reshape(tok_count, head_count, HD)

    query_rows, key_rows, value_rows, output_rows, grad_rows = (
        lax.all_to_all(to_heads(query_proj), "uly", split_axis=1, concat_axis=0, tiled=True),
        lax.all_to_all(to_heads(key_proj), "uly", split_axis=1, concat_axis=0, tiled=True),
        lax.all_to_all(to_heads(value_proj), "uly", split_axis=1, concat_axis=0, tiled=True),
        lax.all_to_all(to_heads(attn_output), "uly", split_axis=1, concat_axis=0, tiled=True),
        lax.all_to_all(to_heads(out_grad), "uly", split_axis=1, concat_axis=0, tiled=True),
    )
    row_delta = jnp.sum(
        output_rows.astype(jnp.float32) * grad_rows.astype(jnp.float32), axis=2
    ).reshape(-1)
    shard_len = query_rows.shape[0]
    per_shard = shard_len // BLOCK
    query_blocks = query_rows.reshape(per_shard, BLOCK, HD)
    key_blocks = key_rows.reshape(per_shard, BLOCK, HD)
    value_blocks = value_rows.reshape(per_shard, BLOCK, HD)
    grad_blocks = grad_rows.reshape(per_shard, BLOCK, HD)
    delta_blocks = row_delta.reshape(per_shard, BLOCK)
    cycle_size = lax.axis_size("blk")
    cycle_rank = lax.axis_index("blk")
    block_count = random_blocks.shape[0]
    grouped, rank_in = named_table(random_blocks, per_shard)
    select, filled = send_slots(grouped, rank_in, cycle_rank, per_shard)
    key_send = jnp.where(
        filled[:, :, None, None],
        jnp.take(key_blocks, select.reshape(-1), axis=0).reshape(cycle_size, CAP, BLOCK, HD),
        jnp.zeros((), jnp.bfloat16),
    )
    value_send = jnp.where(
        filled[:, :, None, None],
        jnp.take(value_blocks, select.reshape(-1), axis=0).reshape(cycle_size, CAP, BLOCK, HD),
        jnp.zeros((), jnp.bfloat16),
    )
    extra_key = jnp.broadcast_to(
        jnp.stack([key_blocks[per_shard - 1], key_blocks[0]])[None], (cycle_size, 2, BLOCK, HD)
    )
    extra_value = jnp.broadcast_to(
        jnp.stack([value_blocks[per_shard - 1], value_blocks[0]])[None], (cycle_size, 2, BLOCK, HD)
    )
    all_key, all_value = (
        lax.all_to_all(
            jnp.concatenate([key_send, extra_key], axis=1),
            "blk",
            split_axis=0,
            concat_axis=0,
            tiled=True,
        ),
        lax.all_to_all(
            jnp.concatenate([value_send, extra_value], axis=1),
            "blk",
            split_axis=0,
            concat_axis=0,
            tiled=True,
        ),
    )
    far_key = all_key[:, :CAP]
    far_value = all_value[:, :CAP]
    before_rank = jnp.maximum(cycle_rank - 1, 0)
    prev_key = lax.dynamic_index_in_dim(all_key, before_rank, 0, keepdims=False)[CAP]
    prev_value = lax.dynamic_index_in_dim(all_value, before_rank, 0, keepdims=False)[CAP]
    first_key = all_key[0, CAP + 1]
    first_value = all_value[0, CAP + 1]
    key_store = jnp.concatenate(
        [key_blocks, prev_key[None], first_key[None], far_key.reshape(cycle_size * CAP, BLOCK, HD)],
        axis=0,
    )
    value_store = jnp.concatenate(
        [
            value_blocks,
            prev_value[None],
            first_value[None],
            far_value.reshape(cycle_size * CAP, BLOCK, HD),
        ],
        axis=0,
    )
    store_size = key_store.shape[0]
    picked = lax.dynamic_slice_in_dim(random_blocks, cycle_rank * per_shard, per_shard, 0)
    own_rank = lax.dynamic_index_in_dim(rank_in, cycle_rank, 0, keepdims=False).reshape(-1)
    all_ids = jnp.arange(block_count, dtype=jnp.int32)
    slot_of = jnp.sum(
        jnp.where(picked[:, :, None] == all_ids[None, None, :], own_rank[None, None, :], 0), axis=2
    )
    owner = picked // per_shard
    random_index = jnp.where(
        owner == cycle_rank, picked - cycle_rank * per_shard, per_shard + 2 + owner * CAP + slot_of
    )
    local_ids = jnp.arange(per_shard, dtype=jnp.int32)
    global_ids = cycle_rank * per_shard + local_ids
    listed = jnp.concatenate(
        [
            global_ids[:, None],
            global_ids[:, None] - 1,
            jnp.zeros((per_shard, 1), jnp.int32),
            picked,
        ],
        axis=1,
    )
    first_index = jnp.zeros((per_shard, 1), jnp.int32) + jnp.where(
        cycle_rank == 0, 0, per_shard + 1
    ).astype(jnp.int32)
    store_index = jnp.concatenate(
        [
            local_ids[:, None],
            jnp.where(local_ids >= 1, local_ids - 1, per_shard)[:, None],
            first_index,
            random_index,
        ],
        axis=1,
    )
    order = jnp.arange(extent, dtype=jnp.int32)
    earlier = order[None, :] < order[:, None]
    repeated = jnp.any((listed[:, :, None] == listed[:, None, :]) & earlier[None, :, :], axis=2)
    usable = (listed >= 0) & jnp.logical_not(repeated)
    within = jnp.arange(BLOCK, dtype=jnp.int32)
    group = math.gcd(per_shard, max(1, 512 // BLOCK))
    group_count = per_shard // group

    def group_turn(carry, group_index):
        key_grad_store, value_grad_store = carry
        first = group_index * group
        query_grp = lax.dynamic_slice_in_dim(query_blocks, first, group, 0)
        grad_grp = lax.dynamic_slice_in_dim(grad_blocks, first, group, 0)
        delta_grp = lax.dynamic_slice_in_dim(delta_blocks, first, group, 0)
        index_grp = lax.dynamic_slice_in_dim(store_index, first, group, 0).reshape(-1)
        listed_grp = lax.dynamic_slice_in_dim(listed, first, group, 0)
        usable_grp = lax.dynamic_slice_in_dim(usable, first, group, 0)
        key_sel = jnp.take(key_store, index_grp, axis=0).reshape(group, extent * BLOCK, HD)
        value_sel = jnp.take(value_store, index_grp, axis=0).reshape(group, extent * BLOCK, HD)
        scores = (
            jnp.einsum("gqd,gkd->gqk", query_grp, key_sel, preferred_element_type=jnp.float32)
            * score_scale
        )
        query_pos = (cycle_rank * per_shard + first + jnp.arange(group, dtype=jnp.int32))[
            :, None
        ] * BLOCK + within[None, :]
        key_pos = (listed_grp[:, :, None] * BLOCK + within[None, None, :]).reshape(
            group, extent * BLOCK
        )
        allowed = jnp.repeat(usable_grp, BLOCK, axis=1)[:, None, :] & (
            key_pos[:, None, :] <= query_pos[:, :, None]
        )
        row_max = jnp.max(jnp.where(allowed, scores, -1e30), axis=2)
        total = jnp.sum(jnp.where(allowed, jnp.exp(scores - row_max[:, :, None]), 0.0), axis=2)
        log_total = row_max + jnp.log(total)
        probs = jnp.where(allowed, jnp.exp(scores - log_total[:, :, None]), 0.0)
        prob_grad = jnp.einsum(
            "gqd,gkd->gqk", grad_grp, value_sel, preferred_element_type=jnp.float32
        )
        score_grad = (probs * (prob_grad - delta_grp[:, :, None]) * score_scale).astype(
            jnp.bfloat16
        )
        query_part = jnp.einsum(
            "gqk,gkd->gqd", score_grad, key_sel, preferred_element_type=jnp.float32
        ).astype(jnp.bfloat16)
        key_part = jnp.einsum(
            "gqk,gqd->gkd", score_grad, query_grp, preferred_element_type=jnp.float32
        )
        value_part = jnp.einsum(
            "gqk,gqd->gkd", probs.astype(jnp.bfloat16), grad_grp, preferred_element_type=jnp.float32
        )
        key_grad_store = key_grad_store.at[index_grp].add(
            key_part.reshape(group * extent, BLOCK, HD)
        )
        value_grad_store = value_grad_store.at[index_grp].add(
            value_part.reshape(group * extent, BLOCK, HD)
        )
        return ((key_grad_store, value_grad_store), query_part)

    zero_store = jnp.zeros((store_size, BLOCK, HD), jnp.float32)
    (key_grad_store, value_grad_store), query_parts = lax.scan(
        group_turn, (zero_store, zero_store), jnp.arange(group_count, dtype=jnp.int32)
    )
    query_acc = query_parts.reshape(shard_len, HD)
    key_acc = key_grad_store[:per_shard]
    value_acc = value_grad_store[:per_shard]
    far_key_grad = key_grad_store[per_shard + 2 :].reshape(cycle_size, CAP, BLOCK, HD)
    far_value_grad = value_grad_store[per_shard + 2 :].reshape(cycle_size, CAP, BLOCK, HD)
    dest_ids = jnp.arange(cycle_size, dtype=jnp.int32)
    to_prev = (dest_ids == cycle_rank - 1)[:, None, None]
    to_first = (dest_ids == 0)[:, None, None]
    extra_key_grad = jnp.stack(
        [
            jnp.where(to_prev, key_grad_store[per_shard][None], 0.0),
            jnp.where(to_first, key_grad_store[per_shard + 1][None], 0.0),
        ],
        axis=1,
    )
    extra_value_grad = jnp.stack(
        [
            jnp.where(to_prev, value_grad_store[per_shard][None], 0.0),
            jnp.where(to_first, value_grad_store[per_shard + 1][None], 0.0),
        ],
        axis=1,
    )
    all_key_back, all_value_back = (
        lax.all_to_all(
            jnp.concatenate([far_key_grad, extra_key_grad], axis=1),
            "blk",
            split_axis=0,
            concat_axis=0,
            tiled=True,
        ),
        lax.all_to_all(
            jnp.concatenate([far_value_grad, extra_value_grad], axis=1),
            "blk",
            split_axis=0,
            concat_axis=0,
            tiled=True,
        ),
    )
    back_key = all_key_back[:, :CAP]
    back_value = all_value_back[:, :CAP]
    prev_back = jnp.stack(
        [jnp.sum(all_key_back[:, CAP], axis=0), jnp.sum(all_value_back[:, CAP], axis=0)]
    )
    first_back = jnp.stack(
        [jnp.sum(all_key_back[:, CAP + 1], axis=0), jnp.sum(all_value_back[:, CAP + 1], axis=0)]
    )
    key_acc = key_acc.at[per_shard - 1].add(prev_back[0]).at[0].add(first_back[0])
    value_acc = value_acc.at[per_shard - 1].add(prev_back[1]).at[0].add(first_back[1])
    back_key = jnp.where(filled[:, :, None, None], back_key, 0.0).reshape(
        cycle_size * CAP, BLOCK, HD
    )
    back_value = jnp.where(filled[:, :, None, None], back_value, 0.0).reshape(
        cycle_size * CAP, BLOCK, HD
    )
    key_acc = key_acc.at[select.reshape(-1)].add(back_key).reshape(shard_len, HD)
    value_acc = value_acc.at[select.reshape(-1)].add(back_value).reshape(shard_len, HD)
    outgoing = (
        query_acc.reshape(shard_len, 1, HD),
        key_acc.astype(jnp.bfloat16).reshape(shard_len, 1, HD),
        value_acc.astype(jnp.bfloat16).reshape(shard_len, 1, HD),
    )
    query_back, key_back, value_back = (
        lax.all_to_all(outgoing[0], "uly", split_axis=0, concat_axis=1, tiled=True),
        lax.all_to_all(outgoing[1], "uly", split_axis=0, concat_axis=1, tiled=True),
        lax.all_to_all(outgoing[2], "uly", split_axis=0, concat_axis=1, tiled=True),
    )
    return (
        query_back.reshape(tok_count, head_count * HD),
        key_back.reshape(tok_count, head_count * HD),
        value_back.reshape(tok_count, head_count * HD),
    )


NEG = -1e30
KEY, QUERY, VALUE, GRAD = 0, 1, 2, 3
ROWS_BY_COLS = (((1,), (1,)), ((), ()))
COLS_BY_COLS = (((0,), (0,)), ((), ()))


def fused_kernel(
    shards,
    uly,
    picks_hbm,
    q_ref,
    k_ref,
    v_ref,
    o_ref,
    g_ref,
    dq_ref,
    dk_ref,
    dv_ref,
    picks_ref,
    rows_in,
    held,
    delta_send,
    delta_recv,
    bias,
    stats,
    scores,
    probs_low,
    score_grads,
    acc,
    outgoing,
    zs,
    zr,
    zl,
    ds_sem,
    dr_sem,
    fs,
    fr,
    ss,
    sr,
    os_sem,
    or_sem,
    ol,
    il,
):
    tok = q_ref.shape[0]
    length = tok * uly
    per = length // BLOCK
    gp = BLOCK // tok
    blocks = per * shards
    scale = HD ** (-0.5)
    b = lax.axis_index("blk")
    u = lax.axis_index("uly")
    inputs = {KEY: k_ref, QUERY: q_ref, VALUE: v_ref, GRAD: g_ref}
    f32 = jnp.float32

    def peer(step):
        return lax.rem(u + step, uly)

    def swap_order(count, at=None):
        at = u if at is None else at
        if count & (count - 1):
            return [lax.rem(at + step, count) for step in range(1, count)]
        order = []
        for mask in range(1, count):
            other = at
            for bit in range(count.bit_length() - 1):
                if mask >> bit & 1:
                    other = other + (1 << bit) * (1 - 2 * (at // (1 << bit) % 2))
            order.append(other)
        return order

    def cols(p):
        return pl.ds(pl.multiple_of(p * HD, HD), HD)

    def rows(p):
        return pl.ds(pl.multiple_of(p * tok, tok), tok)

    def block_rows(c):
        return pl.ds(pl.multiple_of(c * BLOCK, BLOCK), BLOCK)

    def z_copy(t, p, sender):
        return pltpu.make_async_remote_copy(
            src_ref=inputs[t].at[:, cols(p)],
            dst_ref=held.at[t, b, rows(sender), :],
            send_sem=zs.at[t, p],
            recv_sem=zr.at[t, sender],
            device_id={"blk": b, "uly": p},
            device_id_type=pl.DeviceIdType.MESH,
        )

    def d_copy(p, sender):
        return pltpu.make_async_remote_copy(
            src_ref=delta_send.at[p],
            dst_ref=delta_recv.at[sender],
            send_sem=ds_sem.at[p],
            recv_sem=dr_sem.at[sender],
            device_id={"blk": b, "uly": p},
            device_id_type=pl.DeviceIdType.MESH,
        )

    def f_copy(t, c, to, sender):
        return pltpu.make_async_remote_copy(
            src_ref=held.at[t, sender, block_rows(c), :],
            dst_ref=held.at[t, sender, block_rows(c), :],
            send_sem=fs.at[t, c, to],
            recv_sem=fr.at[t, c, sender],
            device_id={"blk": to, "uly": u},
            device_id_type=pl.DeviceIdType.MESH,
        )

    def s_copy(to, sender):
        return pltpu.make_async_remote_copy(
            src_ref=stats.at[sender],
            dst_ref=stats.at[sender],
            send_sem=ss.at[to],
            recv_sem=sr.at[sender],
            device_id={"blk": to, "uly": u},
            device_id_type=pl.DeviceIdType.MESH,
        )

    results = (dq_ref, dk_ref, dv_ref)

    def o_copy(t, p, sender):
        return pltpu.make_async_remote_copy(
            src_ref=outgoing.at[t, rows(p), :],
            dst_ref=results[t].at[:, cols(sender)],
            send_sem=os_sem.at[t, p],
            recv_sem=or_sem.at[t, sender],
            device_id={"blk": b, "uly": p},
            device_id_type=pl.DeviceIdType.MESH,
        )

    def o_local(t):
        return pltpu.make_async_copy(
            outgoing.at[t, rows(u), :], results[t].at[:, cols(u)], ol.at[t]
        )

    def z_local(t):
        return pltpu.make_async_copy(inputs[t].at[:, cols(u)], held.at[t, b, rows(u), :], zl.at[t])

    fetches = (
        pltpu.make_async_copy(o_ref, rows_in.at[0], il.at[0]),
        pltpu.make_async_copy(g_ref, rows_in.at[1], il.at[1]),
        pltpu.make_async_copy(picks_hbm, picks_ref, il.at[2]),
    )
    for fetch in fetches:
        fetch.start()
    barrier = pltpu.get_barrier_semaphore()
    for step in range(1, uly):
        pl.semaphore_signal(
            barrier,
            inc=1,
            device_id={"blk": b, "uly": peer(step)},
            device_id_type=pl.DeviceIdType.MESH,
        )
    for step in range(1, shards):
        pl.semaphore_signal(
            barrier,
            inc=1,
            device_id={"blk": lax.rem(b + step, shards), "uly": u},
            device_id_type=pl.DeviceIdType.MESH,
        )
    for fetch in fetches:
        fetch.wait()
    product = rows_in[0].astype(f32) * rows_in[1].astype(f32)
    high = product.astype(jnp.bfloat16)
    low = (product - high.astype(f32)).astype(jnp.bfloat16)
    head_of = lax.broadcasted_iota(jnp.int32, (uly, uly * HD), 1) // HD
    pick_head = jnp.where(
        head_of == lax.broadcasted_iota(jnp.int32, (uly, uly * HD), 0), 1.0, 0.0
    ).astype(jnp.bfloat16)
    sums = lax.dot_general(
        pick_head, jnp.concatenate([high] * gp, axis=0), ROWS_BY_COLS, preferred_element_type=f32
    ) + lax.dot_general(
        pick_head, jnp.concatenate([low] * gp, axis=0), ROWS_BY_COLS, preferred_element_type=f32
    )
    place = lax.broadcasted_iota(jnp.int32, (uly, BLOCK), 1) // tok
    sums = jnp.where(place == lax.rem(u, gp), sums, 0.0)
    for head in range(uly):
        delta_send[head] = sums[head : head + 1]
    delta_recv[u] = delta_send[u]

    lane_block = lax.broadcasted_iota(jnp.int32, (1, length), 1) // BLOCK
    key_block = lax.broadcasted_iota(jnp.int32, (blocks, length), 0)
    for s in range(shards):
        query_block = lane_block + s * per
        hit = (key_block == query_block) | (key_block == query_block - 1) | (key_block == 0)
        for r in range(RAND):
            named = jnp.zeros((1, length), jnp.int32)
            for i in range(per):
                named = jnp.where(lane_block == i, picks_ref[r, s * per + i], named)
            hit = hit | (key_block == named)
        hit = hit & (key_block <= query_block)
        bias[s] = jnp.where(hit, 0.0, NEG)

    pl.semaphore_wait(barrier, uly - 1 + shards - 1)
    z_order = swap_order(uly)
    for pair in ((KEY, QUERY), (VALUE, GRAD)):
        for t in pair:
            z_local(t).start()
        for p in z_order:
            for t in pair:
                z_copy(t, p, u).start()
    for p in z_order:
        d_copy(p, u).start()

    own_block = u // gp

    def forward(pair):
        for t in pair:
            z_local(t).wait()
        for c in [own_block] + swap_order(per, own_block):
            for t in pair:
                for i in range(gp):
                    p = c * gp + i

                    @pl.when(p != u)
                    def _():
                        z_copy(t, p, p).wait_recv()

                for to in range(shards):
                    goes = (to > b) if t in (KEY, VALUE) else (to < b)

                    @pl.when(goes)
                    def _():
                        f_copy(t, c, to, b).start()

    def tile_scores(s_key, s_query, jb):
        keys = held[KEY, s_key, pl.ds(jb * BLOCK, BLOCK), :]
        tile = lax.dot_general(
            keys, held[QUERY, s_query], ROWS_BY_COLS, preferred_element_type=f32
        )
        return tile * scale + bias[s_query, pl.ds(s_key * per + jb, 1), :]

    forward((KEY, QUERY))

    top = jnp.full((1, length), NEG, f32)
    for jb in range(per):
        tile = tile_scores(b, b, jb)
        key_at = lax.broadcasted_iota(jnp.int32, (BLOCK, length), 0) + jb * BLOCK
        query_at = lax.broadcasted_iota(jnp.int32, (BLOCK, length), 1)
        tile = jnp.where(key_at <= query_at, tile, NEG)
        scores[b, pl.ds(jb * BLOCK, BLOCK), :] = tile
        top = jnp.maximum(top, jnp.max(tile, axis=0, keepdims=True))

    forward((VALUE, GRAD))

    def far_scores(s, top):
        for jb in range(per):
            f_copy(KEY, jb, b, s).wait_recv()
            tile = tile_scores(s, b, jb)
            scores[s, pl.ds(jb * BLOCK, BLOCK), :] = tile
            top = jnp.maximum(top, jnp.max(tile, axis=0, keepdims=True))
        return top

    top = lax.fori_loop(0, b, far_scores, top)

    def add_exp(s, total):
        for jb in range(per):
            tile = jnp.exp(scores[s, pl.ds(jb * BLOCK, BLOCK), :] - top)
            total = total + jnp.sum(tile, axis=0, keepdims=True)
        return total

    total = lax.fori_loop(0, b + 1, add_exp, jnp.zeros((1, length), f32))
    log_total = top + jnp.log(total)
    for step in range(1, uly):
        d_copy(peer(step), peer(step)).wait_recv()
    pieces = []
    for c in range(per):
        piece = delta_recv[c * gp]
        for i in range(1, gp):
            piece = piece + delta_recv[c * gp + i]
        pieces.append(piece)
    delta = jnp.concatenate(pieces, axis=1)
    stats[b, 0:1, :] = log_total
    stats[b, 1:2, :] = delta
    for to in range(shards):

        @pl.when(to < b)
        def _():
            s_copy(to, b).start()

    def tile_grads(tile, s_key, s_query, jb, log_row, delta_row):
        probs = jnp.exp(tile - log_row)
        values = held[VALUE, s_key, pl.ds(jb * BLOCK, BLOCK), :]
        prob_grad = lax.dot_general(
            values, held[GRAD, s_query], ROWS_BY_COLS, preferred_element_type=f32
        )
        grads = (probs * (prob_grad - delta_row) * scale).astype(jnp.bfloat16)
        return probs.astype(jnp.bfloat16), grads

    for jb in range(per):
        probs, grads = tile_grads(
            scores[b, pl.ds(jb * BLOCK, BLOCK), :], b, b, jb, log_total, delta
        )
        probs_low[pl.ds(jb * BLOCK, BLOCK), :] = probs
        score_grads[pl.ds(jb * BLOCK, BLOCK), :] = grads
    acc[0] = lax.dot_general(
        score_grads[...], held[KEY, b], COLS_BY_COLS, preferred_element_type=f32
    )
    acc[1] = jnp.dot(score_grads[...], held[QUERY, b], preferred_element_type=f32)
    acc[2] = jnp.dot(probs_low[...], held[GRAD, b], preferred_element_type=f32)

    def send_result(t):
        outgoing[t] = acc[t].astype(jnp.bfloat16)
        for p in z_order:
            o_copy(t, p, u).start()
        o_local(t).start()

    @pl.when(b == shards - 1)
    def _():
        send_result(1)
        send_result(2)

    def far_keys(s, carry):
        for jb in range(per):
            f_copy(VALUE, jb, b, s).wait_recv()
            _, grads = tile_grads(
                scores[s, pl.ds(jb * BLOCK, BLOCK), :], s, b, jb, log_total, delta
            )
            score_grads[pl.ds(jb * BLOCK, BLOCK), :] = grads
        acc[0] += lax.dot_general(
            score_grads[...], held[KEY, s], COLS_BY_COLS, preferred_element_type=f32
        )
        return carry

    lax.fori_loop(0, b, far_keys, 0)

    send_result(0)

    def far_queries(s, carry):
        for c in range(per):
            f_copy(QUERY, c, b, s).wait_recv()
            f_copy(GRAD, c, b, s).wait_recv()
        s_copy(b, s).wait_recv()
        log_row = stats[s, 0:1, :]
        delta_row = stats[s, 1:2, :]
        for jb in range(per):
            probs, grads = tile_grads(tile_scores(b, s, jb), b, s, jb, log_row, delta_row)
            probs_low[pl.ds(jb * BLOCK, BLOCK), :] = probs
            score_grads[pl.ds(jb * BLOCK, BLOCK), :] = grads
        acc[1] += jnp.dot(score_grads[...], held[QUERY, s], preferred_element_type=f32)
        acc[2] += jnp.dot(probs_low[...], held[GRAD, s], preferred_element_type=f32)
        return carry

    @pl.when(b < shards - 1)
    def _():
        lax.fori_loop(b + 1, shards, far_queries, 0)
        send_result(1)
        send_result(2)


    for step in range(1, uly):
        p = peer(step)
        d_copy(p, u).wait_send()
        for t in (KEY, QUERY, VALUE, GRAD):
            z_copy(t, p, u).wait_send()
    for to in range(shards):

        @pl.when(to > b)
        def _():
            for c in range(per):
                f_copy(KEY, c, to, b).wait_send()
                f_copy(VALUE, c, to, b).wait_send()

        @pl.when(to < b)
        def _():
            for c in range(per):
                f_copy(QUERY, c, to, b).wait_send()
                f_copy(GRAD, c, to, b).wait_send()
            s_copy(to, b).wait_send()

    for t in range(3):
        o_local(t).wait()
        for step in range(1, uly):
            p = peer(step)
            o_copy(t, p, p).wait_recv()
            o_copy(t, p, u).wait_send()


def write_out(a_ref, b_ref, c_ref, a_out, b_out, c_out, held, arrived, done):
    pairs = ((a_ref, a_out), (b_ref, b_out), (c_ref, c_out))
    reads = [
        pltpu.make_async_copy(source, held.at[i], arrived.at[i])
        for i, (source, _) in enumerate(pairs)
    ]
    writes = [
        pltpu.make_async_copy(held.at[i], target, done.at[i])
        for i, (_, target) in enumerate(pairs)
    ]
    for read in reads:
        read.start()
    for read, write in zip(reads, writes):
        read.wait()
        write.start()
    for write in writes:
        write.wait()


def fused_on_device(shards, uly, q, k, v, o, g, random_blocks):
    tok, width = q.shape
    length = tok * uly
    per = length // BLOCK
    dma = pltpu.SemaphoreType.DMA
    hbm = pl.BlockSpec(memory_space=pltpu.HBM)
    results = pl.pallas_call(
        functools.partial(fused_kernel, shards, uly),
        out_shape=[jax.ShapeDtypeStruct((tok, width), jnp.bfloat16)] * 3,
        in_specs=[hbm] * 6,
        out_specs=[hbm] * 3,
        scratch_shapes=[
            pltpu.SMEM(random_blocks.shape[::-1], jnp.int32),
            pltpu.VMEM((2, tok, width), jnp.bfloat16),
            pltpu.VMEM((4, shards, length, HD), jnp.bfloat16),
            pltpu.VMEM((uly, 1, BLOCK), jnp.float32),
            pltpu.VMEM((uly, 1, BLOCK), jnp.float32),
            pltpu.VMEM((shards, shards * per, length), jnp.float32),
            pltpu.VMEM((shards, 2, length), jnp.float32),
            pltpu.VMEM((shards, length, length), jnp.float32),
            pltpu.VMEM((length, length), jnp.bfloat16),
            pltpu.VMEM((length, length), jnp.bfloat16),
            pltpu.VMEM((3, length, HD), jnp.float32),
            pltpu.VMEM((3, length, HD), jnp.bfloat16),
            dma((4, uly)),
            dma((4, uly)),
            dma((4,)),
            dma((uly,)),
            dma((uly,)),
            dma((4, per, shards)),
            dma((4, per, shards)),
            dma((shards,)),
            dma((shards,)),
            dma((3, uly)),
            dma((3, uly)),
            dma((3,)),
            dma((3,)),
        ],
        compiler_params=pltpu.CompilerParams(
            collective_id=0, has_side_effects=True, vmem_limit_bytes=67043328
        ),
    )(random_blocks.T, q, k, v, o, g)
    return pl.pallas_call(
        write_out,
        out_shape=[jax.ShapeDtypeStruct((tok, width), jnp.bfloat16)] * 3,
        in_specs=[hbm] * 3,
        out_specs=[hbm] * 3,
        scratch_shapes=[pltpu.VMEM((3, tok, width), jnp.bfloat16), dma((3,)), dma((3,))],
        compiler_params=pltpu.CompilerParams(vmem_limit_bytes=67043328),
    )(*results)


def wide_or_fused(shards, uly, *operands):
    tok, width = operands[0].shape
    length = tok * uly
    fits = shards * length * length * 4 <= 16 * 1024 * 1024
    if fits and width == uly * HD and BLOCK % tok == 0 and length % BLOCK == 0:
        return tuple(fused_on_device(shards, uly, *operands))
    return on_device(*operands)


def solution(mesh):
    return jax.shard_map(
        functools.partial(wide_or_fused, mesh.shape["blk"], mesh.shape["uly"]),
        mesh=mesh,
        in_specs=(
            P(("blk", "uly"), None),
            P(("blk", "uly"), None),
            P(("blk", "uly"), None),
            P(("blk", "uly"), None),
            P(("blk", "uly"), None),
            P(),
        ),
        out_specs=(P(("blk", "uly"), None), P(("blk", "uly"), None), P(("blk", "uly"), None)),
        check_vma=False,
    )
```

profile of v0, /device:TPU:0, one launch (start us, length us, event | category | flops | bytes accessed | tf_op | source)
XLA Modules:
  0.0 37.8 jit_solution(10215699688215223282)
XLA Ops:
  0.6 35.4 %shard_map.85 = (bf16[64,1024]{1,0:T(8,128)(2,1)}, bf16[64,1024]{1,0:T(8,128)(2,1)}, bf16[64,1024]{1,0:T(8,128)(2,1)}) custom-call(s32[3,16]{1,0:T(4,128)} %bitcast.1, bf16[64,1024]{1,0:T(8,128)(2,1)} %q_ref.1, bf16[64,1024]{1,0:T(8,128)(2,1)} %k_ref.1, bf16[64,1024]{1,0:T(8,128)(2,1)} %v_ref.1, bf16[64,1024]{1,0:T(8,128)(2,1)} %o_ref.1, bf16[64,1024]{1,0:T(8,128)(2,1)} %g_ref.1), custom_call_target="tpu_custom_call" | custom-call | tf_op jit(solution)/shard_map/pallas_call | solution.py:699
  36.1 1.7 %shard_map.86 = (bf16[64,1024]{1,0:T(8,128)(2,1)}, bf16[64,1024]{1,0:T(8,128)(2,1)}, bf16[64,1024]{1,0:T(8,128)(2,1)}) custom-call(bf16[64,1024]{1,0:T(8,128)(2,1)} %get-tuple-element.6.a_ref, bf16[64,1024]{1,0:T(8,128)(2,1)} %get-tuple-element.7.b_ref, bf16[64,1024]{1,0:T(8,128)(2,1)} %get-tuple-element.8.c_ref), custom_call_target="tpu_custom_call" | custom-call | tf_op jit(solution)/shard_map/pallas_call | solution.py:735
where the time goes:
time: 38 us; the launch traced here: 37.8 us
  Pallas kernels  37.2 us (98%)
  between operations  0.64 us (2%)
    pallas_call x1, Pallas kernels, fused_on_device(): pl.pallas_call(functools.partial(fused_kernel, shards, uly), out_shape=[j...  35.4 us
    pallas_call x1, Pallas kernels, fused_on_device(): pl.pallas_call(write_out, out_shape=[jax.ShapeDtypeStruct((tok, width), j...  1.74 us

commit v1 on v0

v1 whole, which is shorter than its diff:
```python
import functools
import math

import jax
import jax.numpy as jnp
from jax import lax
from jax.experimental import pallas as pl
from jax.experimental.pallas import tpu as pltpu
from jax.sharding import PartitionSpec as P

HD = 128
BLOCK = 128
RAND = 3
CAP = 2


def named_table(random_blocks, per_shard):
    block_count = random_blocks.shape[0]
    shard_count = block_count // per_shard
    entries = random_blocks.reshape(shard_count, per_shard * RAND)
    block_ids = jnp.arange(block_count, dtype=jnp.int32)
    named = jnp.any(entries[:, :, None] == block_ids[None, None, :], axis=1)
    owner = block_ids // per_shard
    named = named & (owner[None, :] != jnp.arange(shard_count, dtype=jnp.int32)[:, None])
    grouped = named.reshape(shard_count, shard_count, per_shard).astype(jnp.int32)
    rank_in = jnp.cumsum(grouped, axis=2) - grouped
    return (grouped, rank_in)


def send_slots(grouped, rank_in, cycle_rank, per_shard):
    mine = lax.dynamic_index_in_dim(grouped, cycle_rank, 1, keepdims=False)
    mine_rank = lax.dynamic_index_in_dim(rank_in, cycle_rank, 1, keepdims=False)
    slot_ids = jnp.arange(CAP, dtype=jnp.int32)
    hit = (mine[:, None, :] == 1) & (mine_rank[:, None, :] == slot_ids[None, :, None])
    positions = jnp.arange(per_shard, dtype=jnp.int32)
    select = jnp.sum(jnp.where(hit, positions[None, None, :], 0), axis=2)
    filled = jnp.any(hit, axis=2)
    return (select, filled)


def on_device(query_proj, key_proj, value_proj, attn_output, out_grad, random_blocks):
    tok_count = query_proj.shape[0]
    head_count = query_proj.shape[1] // HD
    score_scale = HD ** (-0.5)
    extent = 3 + RAND

    def to_heads(tensor):
        return tensor.reshape(tok_count, head_count, HD)

    query_rows, key_rows, value_rows, output_rows, grad_rows = (
        lax.all_to_all(to_heads(query_proj), "uly", split_axis=1, concat_axis=0, tiled=True),
        lax.all_to_all(to_heads(key_proj), "uly", split_axis=1, concat_axis=0, tiled=True),
        lax.all_to_all(to_heads(value_proj), "uly", split_axis=1, concat_axis=0, tiled=True),
        lax.all_to_all(to_heads(attn_output), "uly", split_axis=1, concat_axis=0, tiled=True),
        lax.all_to_all(to_heads(out_grad), "uly", split_axis=1, concat_axis=0, tiled=True),
    )
    row_delta = jnp.sum(
        output_rows.astype(jnp.float32) * grad_rows.astype(jnp.float32), axis=2
    ).reshape(-1)
    shard_len = query_rows.shape[0]
    per_shard = shard_len // BLOCK
    query_blocks = query_rows.reshape(per_shard, BLOCK, HD)
    key_blocks = key_rows.reshape(per_shard, BLOCK, HD)
    value_blocks = value_rows.reshape(per_shard, BLOCK, HD)
    grad_blocks = grad_rows.reshape(per_shard, BLOCK, HD)
    delta_blocks = row_delta.reshape(per_shard, BLOCK)
    cycle_size = lax.axis_size("blk")
    cycle_rank = lax.axis_index("blk")
    block_count = random_blocks.shape[0]
    grouped, rank_in = named_table(random_blocks, per_shard)
    select, filled = send_slots(grouped, rank_in, cycle_rank, per_shard)
    key_send = jnp.where(
        filled[:, :, None, None],
        jnp.take(key_blocks, select.reshape(-1), axis=0).reshape(cycle_size, CAP, BLOCK, HD),
        jnp.zeros((), jnp.bfloat16),
    )
    value_send = jnp.where(
        filled[:, :, None, None],
        jnp.take(value_blocks, select.reshape(-1), axis=0).reshape(cycle_size, CAP, BLOCK, HD),
        jnp.zeros((), jnp.bfloat16),
    )
    extra_key = jnp.broadcast_to(
        jnp.stack([key_blocks[per_shard - 1], key_blocks[0]])[None], (cycle_size, 2, BLOCK, HD)
    )
    extra_value = jnp.broadcast_to(
        jnp.stack([value_blocks[per_shard - 1], value_blocks[0]])[None], (cycle_size, 2, BLOCK, HD)
    )
    all_key, all_value = (
        lax.all_to_all(
            jnp.concatenate([key_send, extra_key], axis=1),
            "blk",
            split_axis=0,
            concat_axis=0,
            tiled=True,
        ),
        lax.all_to_all(
            jnp.concatenate([value_send, extra_value], axis=1),
            "blk",
            split_axis=0,
            concat_axis=0,
            tiled=True,
        ),
    )
    far_key = all_key[:, :CAP]
    far_value = all_value[:, :CAP]
    before_rank = jnp.maximum(cycle_rank - 1, 0)
    prev_key = lax.dynamic_index_in_dim(all_key, before_rank, 0, keepdims=False)[CAP]
    prev_value = lax.dynamic_index_in_dim(all_value, before_rank, 0, keepdims=False)[CAP]
    first_key = all_key[0, CAP + 1]
    first_value = all_value[0, CAP + 1]
    key_store = jnp.concatenate(
        [key_blocks, prev_key[None], first_key[None], far_key.reshape(cycle_size * CAP, BLOCK, HD)],
        axis=0,
    )
    value_store = jnp.concatenate(
        [
            value_blocks,
            prev_value[None],
            first_value[None],
            far_value.reshape(cycle_size * CAP, BLOCK, HD),
        ],
        axis=0,
    )
    store_size = key_store.shape[0]
    picked = lax.dynamic_slice_in_dim(random_blocks, cycle_rank * per_shard, per_shard, 0)
    own_rank = lax.dynamic_index_in_dim(rank_in, cycle_rank, 0, keepdims=False).reshape(-1)
    all_ids = jnp.arange(block_count, dtype=jnp.int32)
    slot_of = jnp.sum(
        jnp.where(picked[:, :, None] == all_ids[None, None, :], own_rank[None, None, :], 0), axis=2
    )
    owner = picked // per_shard
    random_index = jnp.where(
        owner == cycle_rank, picked - cycle_rank * per_shard, per_shard + 2 + owner * CAP + slot_of
    )
    local_ids = jnp.arange(per_shard, dtype=jnp.int32)
    global_ids = cycle_rank * per_shard + local_ids
    listed = jnp.concatenate(
        [
            global_ids[:, None],
            global_ids[:, None] - 1,
            jnp.zeros((per_shard, 1), jnp.int32),
            picked,
        ],
        axis=1,
    )
    first_index = jnp.zeros((per_shard, 1), jnp.int32) + jnp.where(
        cycle_rank == 0, 0, per_shard + 1
    ).astype(jnp.int32)
    store_index = jnp.concatenate(
        [
            local_ids[:, None],
            jnp.where(local_ids >= 1, local_ids - 1, per_shard)[:, None],
            first_index,
            random_index,
        ],
        axis=1,
    )
    order = jnp.arange(extent, dtype=jnp.int32)
    earlier = order[None, :] < order[:, None]
    repeated = jnp.any((listed[:, :, None] == listed[:, None, :]) & earlier[None, :, :], axis=2)
    usable = (listed >= 0) & jnp.logical_not(repeated)
    within = jnp.arange(BLOCK, dtype=jnp.int32)
    group = math.gcd(per_shard, max(1, 512 // BLOCK))
    group_count = per_shard // group

    def group_turn(carry, group_index):
        key_grad_store, value_grad_store = carry
        first = group_index * group
        query_grp = lax.dynamic_slice_in_dim(query_blocks, first, group, 0)
        grad_grp = lax.dynamic_slice_in_dim(grad_blocks, first, group, 0)
        delta_grp = lax.dynamic_slice_in_dim(delta_blocks, first, group, 0)
        index_grp = lax.dynamic_slice_in_dim(store_index, first, group, 0).reshape(-1)
        listed_grp = lax.dynamic_slice_in_dim(listed, first, group, 0)
        usable_grp = lax.dynamic_slice_in_dim(usable, first, group, 0)
        key_sel = jnp.take(key_store, index_grp, axis=0).reshape(group, extent * BLOCK, HD)
        value_sel = jnp.take(value_store, index_grp, axis=0).reshape(group, extent * BLOCK, HD)
        scores = (
            jnp.einsum("gqd,gkd->gqk", query_grp, key_sel, preferred_element_type=jnp.float32)
            * score_scale
        )
        query_pos = (cycle_rank * per_shard + first + jnp.arange(group, dtype=jnp.int32))[
            :, None
        ] * BLOCK + within[None, :]
        key_pos = (listed_grp[:, :, None] * BLOCK + within[None, None, :]).reshape(
            group, extent * BLOCK
        )
        allowed = jnp.repeat(usable_grp, BLOCK, axis=1)[:, None, :] & (
            key_pos[:, None, :] <= query_pos[:, :, None]
        )
        row_max = jnp.max(jnp.where(allowed, scores, -1e30), axis=2)
        total = jnp.sum(jnp.where(allowed, jnp.exp(scores - row_max[:, :, None]), 0.0), axis=2)
        log_total = row_max + jnp.log(total)
        probs = jnp.where(allowed, jnp.exp(scores - log_total[:, :, None]), 0.0)
        prob_grad = jnp.einsum(
            "gqd,gkd->gqk", grad_grp, value_sel, preferred_element_type=jnp.float32
        )
        score_grad = (probs * (prob_grad - delta_grp[:, :, None]) * score_scale).astype(
            jnp.bfloat16
        )
        query_part = jnp.einsum(
            "gqk,gkd->gqd", score_grad, key_sel, preferred_element_type=jnp.float32
        ).astype(jnp.bfloat16)
        key_part = jnp.einsum(
            "gqk,gqd->gkd", score_grad, query_grp, preferred_element_type=jnp.float32
        )
        value_part = jnp.einsum(
            "gqk,gqd->gkd", probs.astype(jnp.bfloat16), grad_grp, preferred_element_type=jnp.float32
        )
        key_grad_store = key_grad_store.at[index_grp].add(
            key_part.reshape(group * extent, BLOCK, HD)
        )
        value_grad_store = value_grad_store.at[index_grp].add(
            value_part.reshape(group * extent, BLOCK, HD)
        )
        return ((key_grad_store, value_grad_store), query_part)

    zero_store = jnp.zeros((store_size, BLOCK, HD), jnp.float32)
    (key_grad_store, value_grad_store), query_parts = lax.scan(
        group_turn, (zero_store, zero_store), jnp.arange(group_count, dtype=jnp.int32)
    )
    query_acc = query_parts.reshape(shard_len, HD)
    key_acc = key_grad_store[:per_shard]
    value_acc = value_grad_store[:per_shard]
    far_key_grad = key_grad_store[per_shard + 2 :].reshape(cycle_size, CAP, BLOCK, HD)
    far_value_grad = value_grad_store[per_shard + 2 :].reshape(cycle_size, CAP, BLOCK, HD)
    dest_ids = jnp.arange(cycle_size, dtype=jnp.int32)
    to_prev = (dest_ids == cycle_rank - 1)[:, None, None]
    to_first = (dest_ids == 0)[:, None, None]
    extra_key_grad = jnp.stack(
        [
            jnp.where(to_prev, key_grad_store[per_shard][None], 0.0),
            jnp.where(to_first, key_grad_store[per_shard + 1][None], 0.0),
        ],
        axis=1,
    )
    extra_value_grad = jnp.stack(
        [
            jnp.where(to_prev, value_grad_store[per_shard][None], 0.0),
            jnp.where(to_first, value_grad_store[per_shard + 1][None], 0.0),
        ],
        axis=1,
    )
    all_key_back, all_value_back = (
        lax.all_to_all(
            jnp.concatenate([far_key_grad, extra_key_grad], axis=1),
            "blk",
            split_axis=0,
            concat_axis=0,
            tiled=True,
        ),
        lax.all_to_all(
            jnp.concatenate([far_value_grad, extra_value_grad], axis=1),
            "blk",
            split_axis=0,
            concat_axis=0,
            tiled=True,
        ),
    )
    back_key = all_key_back[:, :CAP]
    back_value = all_value_back[:, :CAP]
    prev_back = jnp.stack(
        [jnp.sum(all_key_back[:, CAP], axis=0), jnp.sum(all_value_back[:, CAP], axis=0)]
    )
    first_back = jnp.stack(
        [jnp.sum(all_key_back[:, CAP + 1], axis=0), jnp.sum(all_value_back[:, CAP + 1], axis=0)]
    )
    key_acc = key_acc.at[per_shard - 1].add(prev_back[0]).at[0].add(first_back[0])
    value_acc = value_acc.at[per_shard - 1].add(prev_back[1]).at[0].add(first_back[1])
    back_key = jnp.where(filled[:, :, None, None], back_key, 0.0).reshape(
        cycle_size * CAP, BLOCK, HD
    )
    back_value = jnp.where(filled[:, :, None, None], back_value, 0.0).reshape(
        cycle_size * CAP, BLOCK, HD
    )
    key_acc = key_acc.at[select.reshape(-1)].add(back_key).reshape(shard_len, HD)
    value_acc = value_acc.at[select.reshape(-1)].add(back_value).reshape(shard_len, HD)
    outgoing = (
        query_acc.reshape(shard_len, 1, HD),
        key_acc.astype(jnp.bfloat16).reshape(shard_len, 1, HD),
        value_acc.astype(jnp.bfloat16).reshape(shard_len, 1, HD),
    )
    query_back, key_back, value_back = (
        lax.all_to_all(outgoing[0], "uly", split_axis=0, concat_axis=1, tiled=True),
        lax.all_to_all(outgoing[1], "uly", split_axis=0, concat_axis=1, tiled=True),
        lax.all_to_all(outgoing[2], "uly", split_axis=0, concat_axis=1, tiled=True),
    )
    return (
        query_back.reshape(tok_count, head_count * HD),
        key_back.reshape(tok_count, head_count * HD),
        value_back.reshape(tok_count, head_count * HD),
    )


NEG = -1e30
KEY, QUERY, GRAD, VALUE = 0, 1, 2, 3
D_QUERY, D_KEY, D_VALUE = 0, 1, 2
ROWS_BY_COLS = (((1,), (1,)), ((), ()))
COLS_BY_COLS = (((0,), (0,)), ((), ()))


def flip(value, mask, count):
    if count & (count - 1):
        return lax.rem(value + mask, count)
    for bit in range(count.bit_length() - 1):
        if mask >> bit & 1:
            value = value + (1 << bit) * (1 - 2 * (value // (1 << bit) % 2))
    return value


def core_of(shard):
    return (shard + 1) // 2 % 2


def fused_kernel(
    shards,
    uly,
    picks_hbm,
    q_ref,
    k_ref,
    v_ref,
    o_ref,
    g_ref,
    out_ref,
    picks_ref,
    rows_in,
    held,
    delta_send,
    delta_recv,
    bias,
    stats,
    scores,
    probs_low,
    score_grads,
    acc,
    partial,
    outgoing,
    zs,
    zr,
    sb,
    st,
    pt,
    ds_sem,
    dr_sem,
    os_sem,
    or_sem,
    il,
):
    tok = q_ref.shape[0]
    length = tok * uly
    per = length // BLOCK
    gp = BLOCK // tok
    blocks = per * shards
    planes = uly // shards
    base = (uly // 2 - planes) // 2
    scale = HD ** (-0.5)
    f32 = jnp.float32
    b = lax.axis_index("blk")
    u = lax.axis_index("uly")
    uz, core = u // 2, u % 2
    plane = uz - base
    is_home = jnp.logical_and(plane >= 0, plane < planes)
    near = jnp.clip(plane, 0, planes - 1)
    head = b + shards * near
    own_source = jnp.logical_and(is_home, core_of(b) == core)
    inputs = {KEY: k_ref, QUERY: q_ref, VALUE: v_ref, GRAD: g_ref}
    mesh_ids = pl.DeviceIdType.MESH

    def home(h, s):
        return h % shards, (base + h // shards) * 2 + core_of(s)

    sibling = (b, uz * 2 + 1 - core)

    def is_self(place):
        return jnp.logical_and(place[0] == b, place[1] == u)

    def ids(place):
        return {"blk": place[0], "uly": place[1]}

    def cols(p):
        return pl.ds(pl.multiple_of(p * HD, HD), HD)

    def rows(p):
        return pl.ds(pl.multiple_of(p * tok, tok), tok)

    def remote(source, target, send, recv, place):
        return pltpu.make_async_remote_copy(
            src_ref=source,
            dst_ref=target,
            send_sem=send,
            recv_sem=recv,
            device_id=ids(place),
            device_id_type=mesh_ids,
        )

    def ship(source, target, send, recv, place):
        mine = is_self(place)

        @pl.when(jnp.logical_not(mine))
        def _():
            remote(source, target, send, recv, place).start()

        @pl.when(mine)
        def _():
            pltpu.make_async_copy(source, target, recv).start()

    def heads():
        return [flip(head, mask, uly) for mask in reversed(range(uly))]

    def z_send(t):
        for h in heads():
            ship(
                inputs[t].at[:, cols(h)],
                held.at[t, b, rows(u), :],
                zs.at[0],
                zr.at[t, b // 2],
                home(h, b),
            )

    fetches = (
        pltpu.make_async_copy(o_ref, rows_in.at[0], il.at[0]),
        pltpu.make_async_copy(g_ref, rows_in.at[1], il.at[1]),
        pltpu.make_async_copy(picks_hbm, picks_ref, il.at[2]),
    )
    barrier = pltpu.get_barrier_semaphore()

    def greet(place):
        pl.semaphore_signal(barrier, inc=1, device_id=ids(place), device_id_type=mesh_ids)

    with jax.named_scope("greet"):

        @pl.when(is_home)
        def _():
            for j in range(shards // 2):
                s = 2 * j + (core + j) % 2
                for mask in reversed(range(uly)):
                    place = (s, flip(u, mask, uly))
                    pl.when(jnp.logical_not(is_self(place)))(functools.partial(greet, place))
            greet(sibling)

        for fetch in fetches:
            fetch.start()
    with jax.named_scope("barrier"):
        pl.semaphore_wait(
            barrier, uly - jnp.where(own_source, 1, 0) + jnp.where(is_home, 1, 0)
        )
    with jax.named_scope("send_kq"):
        z_send(KEY)
        z_send(QUERY)

    with jax.named_scope("prep"):
        for fetch in fetches:
            fetch.wait()
        product = rows_in[0].astype(f32) * rows_in[1].astype(f32)
        high = product.astype(jnp.bfloat16)
        low = (product - high.astype(f32)).astype(jnp.bfloat16)
        head_of = lax.broadcasted_iota(jnp.int32, (uly, uly * HD), 1) // HD
        pick_head = jnp.where(
            head_of == lax.broadcasted_iota(jnp.int32, (uly, uly * HD), 0), 1.0, 0.0
        ).astype(jnp.bfloat16)
        sums = sum(
            lax.dot_general(
                pick_head,
                jnp.concatenate([part] * gp, axis=0),
                ROWS_BY_COLS,
                preferred_element_type=f32,
            )
            for part in (high, low)
        )
        place_of = lax.broadcasted_iota(jnp.int32, (uly, BLOCK), 1) // tok
        sums = jnp.where(place_of == lax.rem(u, gp), sums, 0.0)
        for h in range(uly):
            delta_send[h] = sums[h : h + 1]

    with jax.named_scope("send_gv"):
        for h in heads():
            ship(
                delta_send.at[h], delta_recv.at[b // 2, u], ds_sem.at[0], dr_sem.at[0], home(h, b)
            )
        z_send(GRAD)
        z_send(VALUE)

    def at(jb):
        return pl.ds(jb * BLOCK, BLOCK)

    def run_home(c):
        owned = [s for s in range(shards) if core_of(s) == c]
        foreign = [s for s in range(shards) if core_of(s) != c and s > owned[0]]
        lent = [s for s in owned if any(core_of(k) != c and k < s for k in range(shards))]
        tiles = [(q, k) for k in owned for q in range(k, shards)]
        slot = {tile: n for n, tile in enumerate(tiles)}
        q_all = sorted({q for q, _ in tiles})
        q_own = [q for q in q_all if q in owned]
        q_far = [q for q in q_all if q not in owned]
        pair_of = {QUERY: 0, GRAD: 1}

        def own(t):
            with jax.named_scope(f"own_{t}"):
                for s in owned:
                    ref = held.at[t, s]
                    remote(ref, ref, zs.at[0], zr.at[t, s // 2], (b, u)).wait_recv()
                    if t in pair_of and s in lent:
                        sem = sb.at[pair_of[t], s]
                        remote(ref, ref, sem, sem, sibling).start()

        def lent_copy(t, s):
            sem = sb.at[pair_of[t], s]
            return remote(held.at[t, s], held.at[t, s], sem, sem, sibling)

        def tile_first(q, k, jb):
            return jb * BLOCK if q == k else 0

        def widen(row, first, fill):
            if first:
                return jnp.concatenate([jnp.full((1, first), fill, f32), row], axis=1)
            return row

        def make_scores(q, k, top):
            with jax.named_scope(f"scores_{q}_{k}"):
                for jb in range(per):
                    first = tile_first(q, k, jb)
                    tile = lax.dot_general(
                        held[KEY, k, at(jb), :],
                        held[QUERY, q, first:, :],
                        ROWS_BY_COLS,
                        preferred_element_type=f32,
                    )
                    tile = tile * scale + bias[q, pl.ds(k * per + jb, 1), first:]
                    if q == k:
                        wide = length - first
                        key_at = lax.broadcasted_iota(jnp.int32, (BLOCK, wide), 0)
                        query_at = lax.broadcasted_iota(jnp.int32, (BLOCK, wide), 1)
                        tile = jnp.where(key_at <= query_at, tile, NEG)
                    scores[slot[q, k], at(jb), first:] = tile
                    high = widen(jnp.max(tile, axis=0, keepdims=True), first, NEG)
                    top = high if top is None else jnp.maximum(top, high)
            return top

        def make_exps(q, top):
            with jax.named_scope(f"exps_{q}"):
                total = jnp.zeros((1, length), f32)
                for k in owned:
                    if k > q:
                        continue
                    for jb in range(per):
                        first = tile_first(q, k, jb)
                        tile = jnp.exp(scores[slot[q, k], at(jb), first:] - top[:, first:])
                        scores[slot[q, k], at(jb), first:] = tile
                        part = jnp.sum(tile, axis=0, keepdims=True)
                        total = total + widen(part, first, 0.0)
                stats[c, q, 0:1, :] = top
                stats[c, q, 1:2, :] = total

        def make_probs(q, k, factor):
            with jax.named_scope(f"probs_{q}_{k}"):
                for jb in range(per):
                    first = tile_first(q, k, jb)
                    probs = scores[slot[q, k], at(jb), first:] * factor[:, first:]
                    if first:
                        blank = jnp.zeros((BLOCK, first), jnp.bfloat16)
                        probs_low[slot[q, k], at(jb), :first] = blank
                    probs_low[slot[q, k], at(jb), first:] = probs.astype(jnp.bfloat16)

        def add(ref, value, fresh):
            if fresh:
                ref[...] = value
            else:
                ref[...] += value

        def make_values(q, k, fresh):
            with jax.named_scope(f"values_{q}_{k}"):
                product = jnp.dot(
                    probs_low[slot[q, k]], held[GRAD, q], preferred_element_type=f32
                )
                add(acc.at[D_VALUE, k], product, fresh)

        def make_grads(q, k, factor, delta):
            with jax.named_scope(f"grads_{q}_{k}"):
                for jb in range(per):
                    first = tile_first(q, k, jb)
                    prob_grad = lax.dot_general(
                        held[VALUE, k, at(jb), :],
                        held[GRAD, q, first:, :],
                        ROWS_BY_COLS,
                        preferred_element_type=f32,
                    )
                    grads = (scores[slot[q, k], at(jb), first:] * factor[:, first:]) * (
                        prob_grad - delta[:, first:]
                    )
                    if first:
                        score_grads[at(jb), :first] = jnp.zeros((BLOCK, first), jnp.bfloat16)
                    score_grads[at(jb), first:] = grads.astype(jnp.bfloat16)

        def add_query(q, k, fresh):
            product = lax.dot_general(
                score_grads[...], held[KEY, k], COLS_BY_COLS, preferred_element_type=f32
            )
            add(acc.at[D_QUERY, q], product, fresh)

        def add_key(q, k, fresh):
            product = jnp.dot(score_grads[...], held[QUERY, q], preferred_element_type=f32)
            add(acc.at[D_KEY, k], product, fresh)

        def send_result(t, s):
            with jax.named_scope(f"send_{t}_{s}"):
                outgoing[t, s // 2] = acc[t, s].astype(jnp.bfloat16)
                for mask in list(range(1, uly)) + [0]:
                    p = flip(u, mask, uly)
                    ship(
                        outgoing.at[t, s // 2, rows(p), :],
                        out_ref.at[t, :, cols(head)],
                        os_sem.at[0],
                        or_sem.at[0],
                        (s, p),
                    )

        own(KEY)
        own(QUERY)
        tops = {}
        for q in q_own:
            for k in owned:
                if k <= q:
                    tops[q] = make_scores(q, k, tops.get(q))
        for q in q_own:
            make_exps(q, tops[q])
        for q in q_far:
            with jax.named_scope("lent_q"):
                lent_copy(QUERY, q).wait_recv()
            for k in owned:
                if k <= q:
                    tops[q] = make_scores(q, k, tops.get(q))
            make_exps(q, tops[q])
        with jax.named_scope("stats"):
            remote(delta_recv, delta_recv, ds_sem.at[0], dr_sem.at[0], (b, u)).wait_recv()
            for s in owned:
                pieces = []
                for n in range(per):
                    piece = delta_recv[s // 2, n * gp]
                    for i in range(1, gp):
                        piece = piece + delta_recv[s // 2, n * gp + i]
                    pieces.append(piece)
                stats[c, s, 2:3, :] = jnp.concatenate(pieces, axis=1)
            remote(stats.at[c], stats.at[c], st.at[c], st.at[c], sibling).start()
        own(GRAD)
        with jax.named_scope("stats_wait"):
            remote(stats.at[1 - c], stats.at[1 - c], st.at[c], st.at[1 - c], sibling).wait_recv()
        factors, deltas = {}, {}
        for q in q_all:
            top, total = stats[c, q, 0:1, :], stats[c, q, 1:2, :]
            if any(core_of(k) != c for k in range(q + 1)):
                top_far, total_far = stats[1 - c, q, 0:1, :], stats[1 - c, q, 1:2, :]
                high = jnp.maximum(top, top_far)
                share = jnp.exp(top - high)
                factors[q] = share / (share * total + jnp.exp(top_far - high) * total_far)
            else:
                factors[q] = 1.0 / total
            deltas[q] = stats[c if q in owned else 1 - c, q, 2:3, :]
        for q, k in tiles:
            make_probs(q, k, factors[q])
        fresh = {}
        for q in q_own + q_far:
            if q in q_far:
                with jax.named_scope("lent_g"):
                    lent_copy(GRAD, q).wait_recv()
            for k in owned:
                if k <= q:
                    make_values(q, k, fresh.setdefault(("v", k), True))
                    fresh["v", k] = False
        for k in owned:
            send_result(D_VALUE, k)
        own(VALUE)
        for q in q_far + q_own:
            for k in owned:
                if k <= q:
                    make_grads(q, k, factors[q] * scale, deltas[q])
                    with jax.named_scope(f"dots_{q}_{k}"):
                        add_query(q, k, fresh.setdefault(("q", q), True))
                        add_key(q, k, fresh.setdefault(("k", k), True))
                    fresh["q", q] = fresh["k", k] = False
            if q in q_far:
                ref = acc.at[D_QUERY, q]
                remote(ref, partial.at[q], pt.at[q], pt.at[q], sibling).start()
        for k in owned:
            send_result(D_KEY, k)
        for q in owned:
            if q in lent:
                with jax.named_scope("partial"):
                    ref = partial.at[q]
                    remote(ref, ref, pt.at[q], pt.at[q], sibling).wait_recv()
                    acc[D_QUERY, q] += partial[q]
            send_result(D_QUERY, q)
        with jax.named_scope("lent_sent"):
            for s in lent:
                for t in pair_of:
                    lent_copy(t, s).wait_send()
            for q in q_far:
                ref = acc.at[D_QUERY, q]
                remote(ref, ref, pt.at[q], pt.at[q], sibling).wait_send()
            remote(stats.at[c], stats.at[c], st.at[c], st.at[c], sibling).wait_send()

    @pl.when(is_home)
    def _():
        with jax.named_scope("bias"):
            lane_block = lax.broadcasted_iota(jnp.int32, (1, length), 1) // BLOCK
            key_block = lax.broadcasted_iota(jnp.int32, (blocks, length), 0)
            for s in range(shards):
                query_block = lane_block + s * per
                hit = (key_block == query_block) | (key_block == query_block - 1)
                hit = hit | (key_block == 0)
                for r in range(RAND):
                    named = jnp.zeros((1, length), jnp.int32)
                    for i in range(per):
                        named = jnp.where(lane_block == i, picks_ref[r, s * per + i], named)
                    hit = hit | (key_block == named)
                hit = hit & (key_block <= query_block)
                bias[s] = jnp.where(hit, 0.0, NEG)
        for c in range(2):
            pl.when(core == c)(functools.partial(run_home, c))

    def drain(count):
        ref = held.at[:, 0, pl.ds(0, count * tok), :]
        remote(ref, ref, zs.at[0], zr.at[0, 0], (b, u)).wait_send()
        ref = delta_send.at[pl.ds(0, count)]
        remote(ref, ref, ds_sem.at[0], dr_sem.at[0], (b, u)).wait_send()

    with jax.named_scope("sent"):
        pl.when(own_source)(lambda: drain(uly - 1))
        pl.when(jnp.logical_not(own_source))(lambda: drain(uly))

        @pl.when(own_source)
        def _():
            ref = outgoing.at[:, :, pl.ds(0, length - tok // (shards // 2)), :]
            remote(ref, ref, os_sem.at[0], or_sem.at[0], (b, u)).wait_send()

        @pl.when(jnp.logical_and(is_home, jnp.logical_not(own_source)))
        def _():
            remote(outgoing, outgoing, os_sem.at[0], or_sem.at[0], (b, u)).wait_send()

    with jax.named_scope("landed"):
        remote(out_ref, out_ref, os_sem.at[0], or_sem.at[0], (b, u)).wait_recv()


def write_out(held, a_out, b_out, c_out, done):
    writes = [
        pltpu.make_async_copy(held.at[i], target, done.at[i])
        for i, target in enumerate((a_out, b_out, c_out))
    ]
    for write in writes:
        write.start()
    for write in writes:
        write.wait()


def fused_on_device(shards, uly, q, k, v, o, g, random_blocks):
    tok, width = q.shape
    length = tok * uly
    per = length // BLOCK
    half = shards // 2
    tiles = max(
        sum(shards - k for k in range(shards) if core_of(k) == core) for core in range(2)
    )
    dma = pltpu.SemaphoreType.DMA
    hbm = pl.BlockSpec(memory_space=pltpu.HBM)
    vmem = pl.BlockSpec(memory_space=pltpu.VMEM)
    placed = [
        pltpu.with_memory_space_constraint(x, pltpu.HBM) for x in (random_blocks.T, q, k, v, o, g)
    ]
    results = pl.pallas_call(
        functools.partial(fused_kernel, shards, uly),
        out_shape=jax.ShapeDtypeStruct((3, tok, width), jnp.bfloat16),
        in_specs=[hbm] * 6,
        out_specs=vmem,
        scratch_shapes=[
            pltpu.SMEM(random_blocks.shape[::-1], jnp.int32),
            pltpu.VMEM((2, tok, width), jnp.bfloat16),
            pltpu.VMEM((4, shards, length, HD), jnp.bfloat16),
            pltpu.VMEM((uly, 1, BLOCK), jnp.float32),
            pltpu.VMEM((half, uly, 1, BLOCK), jnp.float32),
            pltpu.VMEM((shards, shards * per, length), jnp.float32),
            pltpu.VMEM((2, shards, 3, length), jnp.float32),
            pltpu.VMEM((tiles, length, length), jnp.float32),
            pltpu.VMEM((tiles, length, length), jnp.bfloat16),
            pltpu.VMEM((length, length), jnp.bfloat16),
            pltpu.VMEM((3, shards, length, HD), jnp.float32),
            pltpu.VMEM((shards, length, HD), jnp.float32),
            pltpu.VMEM((3, half, length, HD), jnp.bfloat16),
            dma((1,)),
            dma((4, half)),
            dma((2, shards)),
            dma((2,)),
            dma((shards,)),
            dma((1,)),
            dma((1,)),
            dma((1,)),
            dma((1,)),
            dma((3,)),
        ],
        compiler_params=pltpu.CompilerParams(
            collective_id=0, has_side_effects=True, vmem_limit_bytes=32 * 1024 * 1024
        ),
    )(*placed)
    return pl.pallas_call(
        write_out,
        out_shape=[jax.ShapeDtypeStruct((tok, width), jnp.bfloat16)] * 3,
        in_specs=[vmem],
        out_specs=[hbm] * 3,
        scratch_shapes=[dma((3,))],
        compiler_params=pltpu.CompilerParams(vmem_limit_bytes=32 * 1024 * 1024),
    )(results)


def wide_or_fused(shards, uly, *operands):
    tok, width = operands[0].shape
    length = tok * uly
    fits = shards * length * length * 4 <= 4 * 1024 * 1024
    paired = shards % 4 == 0 and uly % shards == 0
    if fits and paired and width == uly * HD and BLOCK % tok == 0 and length % BLOCK == 0:
        return tuple(fused_on_device(shards, uly, *operands))
    return on_device(*operands)


def solution(mesh):
    return jax.shard_map(
        functools.partial(wide_or_fused, mesh.shape["blk"], mesh.shape["uly"]),
        mesh=mesh,
        in_specs=(
            P(("blk", "uly"), None),
            P(("blk", "uly"), None),
            P(("blk", "uly"), None),
            P(("blk", "uly"), None),
            P(("blk", "uly"), None),
            P(),
        ),
        out_specs=(P(("blk", "uly"), None), P(("blk", "uly"), None), P(("blk", "uly"), None)),
        check_vma=False,
    )
```

time: 38 us -> 32.1 us (0.84)
  Pallas kernels: 37.2 us -> 31.1 us
    pallas_call x1, Pallas kernels: 35.4 us -> 30.4 us  [fused_on_device(): pl.pallas_call(functools.partial(fused_kernel, shards, uly), out_shape=ja...]
    pallas_call x1, Pallas kernels: 1.74 us -> 0.77 us  [fused_on_device(): pl.pallas_call(write_out, out_shape=[jax.ShapeDtypeStruct((tok, width), j...]
where the time goes in v1:
time: 32.1 us; the launch traced here: 32 us
  Pallas kernels  31.1 us (97%)
  between operations  0.82 us (3%)
    pallas_call x1, Pallas kernels, fused_on_device(): pl.pallas_call(functools.partial(fused_kernel, shards, uly), out_shape=ja...  30.4 us
    pallas_call x1, Pallas kernels, fused_on_device(): pl.pallas_call(write_out, out_shape=[jax.ShapeDtypeStruct((tok, width), j...  0.77 us

profile of v1, /device:TPU:0, one launch (start us, length us, event | category | flops | bytes accessed | tf_op | source)
XLA Modules:
  0.0 32.0 jit_solution(204373253533721594)
XLA Ops:
  0.6 30.4 %shard_map.85.held = bf16[3,64,1024]{2,1,0:T(8,128)(2,1)S(1)} custom-call(s32[3,16]{1,0:T(4,128)} %bitcast.1, bf16[64,1024]{1,0:T(8,128)(2,1)} %q_ref.1, bf16[64,1024]{1,0:T(8,128)(2,1)} %k_ref.1, bf16[64,1024]{1,0:T(8,128)(2,1)} %v_ref.1, bf16[64,1024]{1,0:T(8,128)(2,1)} %o_ref.1, bf16[64,1024]{1,0:T(8,128)(2,1)} %g_ref.1), custom_call_target="tpu_custom_call" | custom-call | tf_op jit(solution)/shard_map/pallas_call | solution.py:767
  31.0 0.8 %shard_map.86 = (bf16[64,1024]{1,0:T(8,128)(2,1)}, bf16[64,1024]{1,0:T(8,128)(2,1)}, bf16[64,1024]{1,0:T(8,128)(2,1)}) custom-call(bf16[3,64,1024]{2,1,0:T(8,128)(2,1)S(1)} %shard_map.85.held), custom_call_target="tpu_custom_call" | custom-call | tf_op jit(solution)/shard_map/pallas_call | solution.py:801

commit v2 on v1

--- a/solution.py
+++ b/solution.py
@@ -392,7 +392,10 @@
             device_id_type=mesh_ids,
         )
 
-    def ship(source, target, send, recv, place):
+    def ship(source, target, send, recv, place, maybe_here):
+        if not maybe_here:
+            remote(source, target, send, recv, place).start()
+            return
         mine = is_self(place)
 
         @pl.when(jnp.logical_not(mine))
@@ -404,16 +407,17 @@
             pltpu.make_async_copy(source, target, recv).start()
 
     def heads():
-        return [flip(head, mask, uly) for mask in reversed(range(uly))]
+        return [(flip(head, mask, uly), mask == 0) for mask in reversed(range(uly))]
 
     def z_send(t):
-        for h in heads():
+        for h, maybe_here in heads():
             ship(
                 inputs[t].at[:, cols(h)],
                 held.at[t, b, rows(u), :],
                 zs.at[0],
                 zr.at[t, b // 2],
                 home(h, b),
+                maybe_here,
             )
 
     fetches = (
@@ -472,9 +476,14 @@
             delta_send[h] = sums[h : h + 1]
 
     with jax.named_scope("send_gv"):
-        for h in heads():
+        for h, maybe_here in heads():
             ship(
-                delta_send.at[h], delta_recv.at[b // 2, u], ds_sem.at[0], dr_sem.at[0], home(h, b)
+                delta_send.at[h],
+                delta_recv.at[b // 2, u],
+                ds_sem.at[0],
+                dr_sem.at[0],
+                home(h, b),
+                maybe_here,
             )
         z_send(GRAD)
         z_send(VALUE)
@@ -611,6 +620,7 @@
                         os_sem.at[0],
                         or_sem.at[0],
                         (s, p),
+                        mask == 0,
                     )
 
         own(KEY)
@@ -654,34 +664,39 @@
             else:
                 factors[q] = 1.0 / total
             deltas[q] = stats[c if q in owned else 1 - c, q, 2:3, :]
-        for q, k in tiles:
-            make_probs(q, k, factors[q])
-        fresh = {}
-        for q in q_own + q_far:
-            if q in q_far:
-                with jax.named_scope("lent_g"):
-                    lent_copy(GRAD, q).wait_recv()
-            for k in owned:
-                if k <= q:
-                    make_values(q, k, fresh.setdefault(("v", k), True))
-                    fresh["v", k] = False
-        for k in owned:
+        started = set()
+
+        def starts(*what):
+            new = what not in started
+            started.add(what)
+            return new
+
+        have = set(q_own)
+        for k in reversed(owned):
+            for q in q_own + q_far:
+                if k > q:
+                    continue
+                make_probs(q, k, factors[q])
+                if q not in have:
+                    with jax.named_scope("lent_g"):
+                        lent_copy(GRAD, q).wait_recv()
+                    have.add(q)
+                make_values(q, k, starts("v", k))
             send_result(D_VALUE, k)
         own(VALUE)
-        for q in q_far + q_own:
-            for k in owned:
-                if k <= q:
-                    make_grads(q, k, factors[q] * scale, deltas[q])
-                    with jax.named_scope(f"dots_{q}_{k}"):
-                        add_query(q, k, fresh.setdefault(("q", q), True))
-                        add_key(q, k, fresh.setdefault(("k", k), True))
-                    fresh["q", q] = fresh["k", k] = False
-            if q in q_far:
-                ref = acc.at[D_QUERY, q]
-                remote(ref, partial.at[q], pt.at[q], pt.at[q], sibling).start()
-        for k in owned:
+        for k in reversed(owned):
+            for q in q_far + q_own:
+                if k > q:
+                    continue
+                make_grads(q, k, factors[q] * scale, deltas[q])
+                with jax.named_scope(f"dots_{q}_{k}"):
+                    add_query(q, k, starts("q", q))
+                    add_key(q, k, starts("k", k))
+                if k == owned[0] and q in q_far:
+                    ref = acc.at[D_QUERY, q]
+                    remote(ref, partial.at[q], pt.at[q], pt.at[q], sibling).start()
             send_result(D_KEY, k)
-        for q in owned:
+        for q in q_own:
             if q in lent:
                 with jax.named_scope("partial"):
                     ref = partial.at[q]

time: 32.1 us -> 31.3 us (0.975)
  Pallas kernels: 31.1 us -> 30.5 us
    pallas_call x1, Pallas kernels: 30.4 us -> 29.7 us  [fused_on_device(): pl.pallas_call(functools.partial(fused_kernel, shards, uly), out_shape=ja...]
where the time goes in v2:
time: 31.3 us; the launch traced here: 31.1 us
  Pallas kernels  30.5 us (97%)
  between operations  0.64 us (2%)
    pallas_call x1, Pallas kernels, fused_on_device(): pl.pallas_call(functools.partial(fused_kernel, shards, uly), out_shape=ja...  29.7 us
    pallas_call x1, Pallas kernels, fused_on_device(): pl.pallas_call(write_out, out_shape=[jax.ShapeDtypeStruct((tok, width), j...  0.77 us

profile of v2, /device:TPU:0, one launch (start us, length us, event | category | flops | bytes accessed | tf_op | source)
XLA Modules:
  0.0 31.1 jit_solution(8124040429949238320)
XLA Ops:
  0.6 29.7 %shard_map.85.held = bf16[3,64,1024]{2,1,0:T(8,128)(2,1)S(1)} custom-call(s32[3,16]{1,0:T(4,128)} %bitcast.1, bf16[64,1024]{1,0:T(8,128)(2,1)} %q_ref.1, bf16[64,1024]{1,0:T(8,128)(2,1)} %k_ref.1, bf16[64,1024]{1,0:T(8,128)(2,1)} %v_ref.1, bf16[64,1024]{1,0:T(8,128)(2,1)} %o_ref.1, bf16[64,1024]{1,0:T(8,128)(2,1)} %g_ref.1), custom_call_target="tpu_custom_call" | custom-call | tf_op jit(solution)/shard_map/pallas_call | solution.py:782
  30.3 0.8 %shard_map.86 = (bf16[64,1024]{1,0:T(8,128)(2,1)}, bf16[64,1024]{1,0:T(8,128)(2,1)}, bf16[64,1024]{1,0:T(8,128)(2,1)}) custom-call(bf16[3,64,1024]{2,1,0:T(8,128)(2,1)S(1)} %shard_map.85.held), custom_call_target="tpu_custom_call" | custom-call | tf_op jit(solution)/shard_map/pallas_call | solution.py:816

commit v3 on v2

--- a/solution.py
+++ b/solution.py
@@ -296,6 +296,9 @@
 D_QUERY, D_KEY, D_VALUE = 0, 1, 2
 ROWS_BY_COLS = (((1,), (1,)), ((), ()))
 COLS_BY_COLS = (((0,), (0,)), ((), ()))
+
+
+FIRST_TILES = ((0, 0), (1, 0), (2, 0), (3, 0), (3, 3), (3, 2), (2, 2), (1, 1), (3, 1), (2, 1))
 
 
 def flip(value, mask, count):
@@ -415,7 +418,7 @@
                 inputs[t].at[:, cols(h)],
                 held.at[t, b, rows(u), :],
                 zs.at[0],
-                zr.at[t, b // 2],
+                zr.at[t, b // 2, u // (uly // 2)],
                 home(h, b),
                 maybe_here,
             )
@@ -501,73 +504,97 @@
         q_own = [q for q in q_all if q in owned]
         q_far = [q for q in q_all if q not in owned]
         pair_of = {QUERY: 0, GRAD: 1}
+        wide = length // 2
 
         def own(t):
             with jax.named_scope(f"own_{t}"):
-                for s in owned:
-                    ref = held.at[t, s]
-                    remote(ref, ref, zs.at[0], zr.at[t, s // 2], (b, u)).wait_recv()
-                    if t in pair_of and s in lent:
-                        sem = sb.at[pair_of[t], s]
-                        remote(ref, ref, sem, sem, sibling).start()
+                for i in range(2):
+                    n = lax.rem(u // (uly // 2) + i, 2)
+                    for s in lent + [s for s in owned if s not in lent]:
+                        ref = held.at[t, s, pl.ds(pl.multiple_of(n * wide, wide), wide), :]
+                        remote(ref, ref, zs.at[0], zr.at[t, s // 2, n], (b, u)).wait_recv()
+                        if t in pair_of and s in lent:
+                            sem = sb.at[pair_of[t], s]
+                            remote(ref, ref, sem, sem, sibling).start()
 
         def lent_copy(t, s):
             sem = sb.at[pair_of[t], s]
             return remote(held.at[t, s], held.at[t, s], sem, sem, sibling)
 
-        def tile_first(q, k, jb):
-            return jb * BLOCK if q == k else 0
-
-        def widen(row, first, fill):
-            if first:
-                return jnp.concatenate([jnp.full((1, first), fill, f32), row], axis=1)
-            return row
-
-        def make_scores(q, k, top):
+        turn = math.log2(math.e) * scale
+
+        def keys_for(q, k, a):
+            return (a + 1) * wide if q == k else length
+
+        def first_lane(q, k, r):
+            return r * wide if q == k else 0
+
+        def lanes(a):
+            return pl.ds(a * wide, wide)
+
+        def fold(tile, op):
+            return op(tile.reshape(tile.shape[0] // 8, 8, tile.shape[1]), axis=0)
+
+        def bias_row(q, k, n, a):
+            return bias[q, pl.ds(k * per + n, 1), lanes(a)]
+
+        def make_scores(q, k, tops):
+            new = []
             with jax.named_scope(f"scores_{q}_{k}"):
-                for jb in range(per):
-                    first = tile_first(q, k, jb)
+                for a in range(2):
+                    count = keys_for(q, k, a)
                     tile = lax.dot_general(
-                        held[KEY, k, at(jb), :],
-                        held[QUERY, q, first:, :],
+                        held[KEY, k, :count, :],
+                        held[QUERY, q, lanes(a), :],
                         ROWS_BY_COLS,
                         preferred_element_type=f32,
                     )
-                    tile = tile * scale + bias[q, pl.ds(k * per + jb, 1), first:]
                     if q == k:
-                        wide = length - first
-                        key_at = lax.broadcasted_iota(jnp.int32, (BLOCK, wide), 0)
-                        query_at = lax.broadcasted_iota(jnp.int32, (BLOCK, wide), 1)
-                        tile = jnp.where(key_at <= query_at, tile, NEG)
-                    scores[slot[q, k], at(jb), first:] = tile
-                    high = widen(jnp.max(tile, axis=0, keepdims=True), first, NEG)
-                    top = high if top is None else jnp.maximum(top, high)
-            return top
-
-        def make_exps(q, top):
+                        key_at = lax.broadcasted_iota(jnp.int32, (wide, wide), 0)
+                        query_at = lax.broadcasted_iota(jnp.int32, (wide, wide), 1)
+                        last = jnp.where(key_at <= query_at, tile[a * wide :], NEG)
+                        tile = jnp.concatenate([tile[: a * wide], last], axis=0) if a else last
+                    scores[slot[q, k], :count, lanes(a)] = tile
+                    top = tops[a] if tops else None
+                    for n in range(count // BLOCK):
+                        part = fold(tile[n * BLOCK : (n + 1) * BLOCK], jnp.max)
+                        part = part * turn + bias_row(q, k, n, a)
+                        top = part if top is None else jnp.maximum(top, part)
+                    new.append(top)
+            return new
+
+        def make_exps(q, tops):
+            totals = []
             with jax.named_scope(f"exps_{q}"):
-                total = jnp.zeros((1, length), f32)
-                for k in owned:
-                    if k > q:
-                        continue
-                    for jb in range(per):
-                        first = tile_first(q, k, jb)
-                        tile = jnp.exp(scores[slot[q, k], at(jb), first:] - top[:, first:])
-                        scores[slot[q, k], at(jb), first:] = tile
-                        part = jnp.sum(tile, axis=0, keepdims=True)
-                        total = total + widen(part, first, 0.0)
-                stats[c, q, 0:1, :] = top
-                stats[c, q, 1:2, :] = total
-
-        def make_probs(q, k, factor):
+                for a in range(2):
+                    top = jnp.max(tops[a], axis=0, keepdims=True)
+                    total = jnp.zeros((8, wide), f32)
+                    for k in owned:
+                        if k > q:
+                            continue
+                        for n in range(keys_for(q, k, a) // BLOCK):
+                            shift = top - bias_row(q, k, n, a)
+                            tile = scores[slot[q, k], at(n), lanes(a)]
+                            tile = jnp.exp2(tile * turn - shift)
+                            scores[slot[q, k], at(n), lanes(a)] = tile
+                            total = total + fold(tile, jnp.sum)
+                    total = jnp.sum(total, axis=0, keepdims=True)
+                    if q in lent or q in q_far:
+                        stats[c, q, 0:1, lanes(a)] = top
+                        stats[c, q, 1:2, lanes(a)] = total
+                    totals.append(total)
+            return jnp.concatenate(totals, axis=1)
+
+        def pieces_of(q, k, start, stop):
+            if q == k and start < wide < stop:
+                return ((start, wide, 0), (wide, stop, wide))
+            return ((start, stop, wide if q == k and start >= wide else 0),)
+
+        def make_probs(q, k, start, stop, factor):
             with jax.named_scope(f"probs_{q}_{k}"):
-                for jb in range(per):
-                    first = tile_first(q, k, jb)
-                    probs = scores[slot[q, k], at(jb), first:] * factor[:, first:]
-                    if first:
-                        blank = jnp.zeros((BLOCK, first), jnp.bfloat16)
-                        probs_low[slot[q, k], at(jb), :first] = blank
-                    probs_low[slot[q, k], at(jb), first:] = probs.astype(jnp.bfloat16)
+                for low, high, first in pieces_of(q, k, start, stop):
+                    probs = scores[slot[q, k], low:high, first:] * factor[:, first:]
+                    probs_low[slot[q, k], low:high, first:] = probs.astype(jnp.bfloat16)
 
         def add(ref, value, fresh):
             if fresh:
@@ -575,70 +602,84 @@
             else:
                 ref[...] += value
 
-        def make_values(q, k, fresh):
+        def make_values(q, k, start, stop, fresh):
             with jax.named_scope(f"values_{q}_{k}"):
-                product = jnp.dot(
-                    probs_low[slot[q, k]], held[GRAD, q], preferred_element_type=f32
-                )
-                add(acc.at[D_VALUE, k], product, fresh)
+                for low, high, first in pieces_of(q, k, start, stop):
+                    product = jnp.dot(
+                        probs_low[slot[q, k], low:high, first:],
+                        held[GRAD, q, first:, :],
+                        preferred_element_type=f32,
+                    )
+                    add(acc.at[D_VALUE, k, low:high, :], product, fresh)
 
         def make_grads(q, k, factor, delta):
             with jax.named_scope(f"grads_{q}_{k}"):
-                for jb in range(per):
-                    first = tile_first(q, k, jb)
+                for a in range(2):
+                    count = keys_for(q, k, a)
                     prob_grad = lax.dot_general(
-                        held[VALUE, k, at(jb), :],
-                        held[GRAD, q, first:, :],
+                        held[VALUE, k, :count, :],
+                        held[GRAD, q, lanes(a), :],
                         ROWS_BY_COLS,
                         preferred_element_type=f32,
                     )
-                    grads = (scores[slot[q, k], at(jb), first:] * factor[:, first:]) * (
-                        prob_grad - delta[:, first:]
+                    span = slice(a * wide, (a + 1) * wide)
+                    grads = (scores[slot[q, k], :count, lanes(a)] * factor[:, span]) * (
+                        prob_grad - delta[:, span]
                     )
-                    if first:
-                        score_grads[at(jb), :first] = jnp.zeros((BLOCK, first), jnp.bfloat16)
-                    score_grads[at(jb), first:] = grads.astype(jnp.bfloat16)
-
-        def add_query(q, k, fresh):
+                    score_grads[:count, lanes(a)] = grads.astype(jnp.bfloat16)
+
+        def add_query(q, k, a, fresh):
+            count = keys_for(q, k, a)
             product = lax.dot_general(
-                score_grads[...], held[KEY, k], COLS_BY_COLS, preferred_element_type=f32
+                score_grads[:count, lanes(a)],
+                held[KEY, k, :count, :],
+                COLS_BY_COLS,
+                preferred_element_type=f32,
             )
-            add(acc.at[D_QUERY, q], product, fresh)
-
-        def add_key(q, k, fresh):
-            product = jnp.dot(score_grads[...], held[QUERY, q], preferred_element_type=f32)
-            add(acc.at[D_KEY, k], product, fresh)
-
-        def send_result(t, s):
-            with jax.named_scope(f"send_{t}_{s}"):
-                outgoing[t, s // 2] = acc[t, s].astype(jnp.bfloat16)
-                for mask in list(range(1, uly)) + [0]:
-                    p = flip(u, mask, uly)
+            add(acc.at[D_QUERY, q, lanes(a), :], product, fresh)
+
+        def add_key(q, k, r, fresh):
+            first = first_lane(q, k, r)
+            product = jnp.dot(
+                score_grads[lanes(r), first:],
+                held[QUERY, q, first:, :],
+                preferred_element_type=f32,
+            )
+            add(acc.at[D_KEY, k, lanes(r), :], product, fresh)
+
+        def send_result(t, s, start=0, stop=length):
+            with jax.named_scope(f"send_{t}_{s}_{start}"):
+                outgoing[t, s // 2, start:stop, :] = acc[t, s, start:stop, :].astype(jnp.bfloat16)
+                inner, outer = 2 * base, 2 * (base + planes)
+                targets = [(p, False) for p in range(uly) if not inner <= p < outer]
+                for mask in reversed(range(outer - inner)):
+                    p = inner + flip(u - inner, mask, outer - inner)
+                    targets.append((p, mask == 0))
+                for p, maybe_here in targets[start // tok : stop // tok]:
                     ship(
                         outgoing.at[t, s // 2, rows(p), :],
                         out_ref.at[t, :, cols(head)],
                         os_sem.at[0],
                         or_sem.at[0],
                         (s, p),
-                        mask == 0,
+                        maybe_here,
                     )
 
         own(KEY)
         own(QUERY)
-        tops = {}
-        for q in q_own:
+        tops, totals = {}, {}
+
+        def all_scores(q):
             for k in owned:
                 if k <= q:
                     tops[q] = make_scores(q, k, tops.get(q))
-        for q in q_own:
-            make_exps(q, tops[q])
-        for q in q_far:
-            with jax.named_scope("lent_q"):
-                lent_copy(QUERY, q).wait_recv()
-            for k in owned:
-                if k <= q:
-                    tops[q] = make_scores(q, k, tops.get(q))
-            make_exps(q, tops[q])
+            totals[q] = make_exps(q, tops[q])
+
+        for q in lent + q_far:
+            if q in q_far:
+                with jax.named_scope("lent_q"):
+                    lent_copy(QUERY, q).wait_recv()
+            all_scores(q)
         with jax.named_scope("stats"):
             remote(delta_recv, delta_recv, ds_sem.at[0], dr_sem.at[0], (b, u)).wait_recv()
             for s in owned:
@@ -650,19 +691,22 @@
                     pieces.append(piece)
                 stats[c, s, 2:3, :] = jnp.concatenate(pieces, axis=1)
             remote(stats.at[c], stats.at[c], st.at[c], st.at[c], sibling).start()
+        for q in q_own:
+            if q not in lent:
+                all_scores(q)
         own(GRAD)
         with jax.named_scope("stats_wait"):
             remote(stats.at[1 - c], stats.at[1 - c], st.at[c], st.at[1 - c], sibling).wait_recv()
         factors, deltas = {}, {}
         for q in q_all:
-            top, total = stats[c, q, 0:1, :], stats[c, q, 1:2, :]
-            if any(core_of(k) != c for k in range(q + 1)):
+            if q in lent or q in q_far:
+                top, total = stats[c, q, 0:1, :], stats[c, q, 1:2, :]
                 top_far, total_far = stats[1 - c, q, 0:1, :], stats[1 - c, q, 1:2, :]
                 high = jnp.maximum(top, top_far)
-                share = jnp.exp(top - high)
-                factors[q] = share / (share * total + jnp.exp(top_far - high) * total_far)
+                share = jnp.exp2(top - high)
+                factors[q] = share / (share * total + jnp.exp2(top_far - high) * total_far)
             else:
-                factors[q] = 1.0 / total
+                factors[q] = 1.0 / totals[q]
             deltas[q] = stats[c if q in owned else 1 - c, q, 2:3, :]
         started = set()
 
@@ -672,37 +716,54 @@
             return new
 
         have = set(q_own)
-        for k in reversed(owned):
-            for q in q_own + q_far:
-                if k > q:
-                    continue
-                make_probs(q, k, factors[q])
-                if q not in have:
-                    with jax.named_scope("lent_g"):
-                        lent_copy(GRAD, q).wait_recv()
-                    have.add(q)
-                make_values(q, k, starts("v", k))
-            send_result(D_VALUE, k)
+        early = min(tok * 2 * base, wide) if c == core_of(0) else 0
+        spans = [(0, early), (early, length)] if early else [(0, length)]
+        for start, stop in spans:
+            for k in owned:
+                queries = [q for q in q_own + q_far if q >= k]
+                for q in queries:
+                    make_probs(q, k, start, stop, factors[q])
+                    if q not in have:
+                        with jax.named_scope("lent_g"):
+                            lent_copy(GRAD, q).wait_recv()
+                        have.add(q)
+                    make_values(q, k, start, stop, q == queries[0])
+                send_result(D_VALUE, k, start, stop)
         own(VALUE)
-        for k in reversed(owned):
-            for q in q_far + q_own:
-                if k > q:
-                    continue
-                make_grads(q, k, factors[q] * scale, deltas[q])
-                with jax.named_scope(f"dots_{q}_{k}"):
-                    add_query(q, k, starts("q", q))
-                    add_key(q, k, starts("k", k))
-                if k == owned[0] and q in q_far:
-                    ref = acc.at[D_QUERY, q]
-                    remote(ref, partial.at[q], pt.at[q], pt.at[q], sibling).start()
-            send_result(D_KEY, k)
-        for q in q_own:
-            if q in lent:
-                with jax.named_scope("partial"):
+        todo = [tile for tile in FIRST_TILES if tile in tiles]
+        todo += [tile for tile in tiles if tile not in todo]
+        waiting = []
+
+        def finish_queries():
+            while waiting:
+                q = waiting.pop(0)
+                with jax.named_scope(f"partial_{q}"):
                     ref = partial.at[q]
                     remote(ref, ref, pt.at[q], pt.at[q], sibling).wait_recv()
                     acc[D_QUERY, q] += partial[q]
-            send_result(D_QUERY, q)
+                send_result(D_QUERY, q)
+
+        while todo:
+            q, k = todo.pop(0)
+            make_grads(q, k, factors[q] * scale, deltas[q])
+            fresh_query, fresh_key = starts("q", q), starts("k", k)
+            with jax.named_scope(f"dots_{q}_{k}"):
+                for a in range(2):
+                    add_query(q, k, a, fresh_query)
+                for r in range(2):
+                    add_key(q, k, r, fresh_key)
+            finish_queries()
+            if all(tile[0] != q for tile in todo):
+                if q in q_far:
+                    ref = acc.at[D_QUERY, q]
+                    remote(ref, partial.at[q], pt.at[q], pt.at[q], sibling).start()
+                elif q in lent:
+                    waiting.append(q)
+                else:
+                    send_result(D_QUERY, q)
+            if all(tile[1] != k for tile in todo):
+                send_result(D_KEY, k)
+        finish_queries()
         with jax.named_scope("lent_sent"):
             for s in lent:
                 for t in pair_of:
@@ -733,7 +794,7 @@
 
     def drain(count):
         ref = held.at[:, 0, pl.ds(0, count * tok), :]
-        remote(ref, ref, zs.at[0], zr.at[0, 0], (b, u)).wait_send()
+        remote(ref, ref, zs.at[0], zr.at[0, 0, 0], (b, u)).wait_send()
         ref = delta_send.at[pl.ds(0, count)]
         remote(ref, ref, ds_sem.at[0], dr_sem.at[0], (b, u)).wait_send()
 
@@ -799,7 +860,7 @@
             pltpu.VMEM((shards, length, HD), jnp.float32),
             pltpu.VMEM((3, half, length, HD), jnp.bfloat16),
             dma((1,)),
-            dma((4, half)),
+            dma((4, half, 2)),
             dma((2, shards)),
             dma((2,)),
             dma((shards,)),

time: 31.3 us -> 29.8 us (0.952); the launches traced: 31.1 us -> 29.2 us
  Pallas kernels: 30.5 us -> 28.6 us
    pallas_call x1, Pallas kernels: 29.7 us -> 27.8 us  [fused_on_device(): pl.pallas_call(functools.partial(fused_kernel, shards, uly), out_shape=ja...]
where the time goes in v3:
time: 29.8 us; the launch traced here: 29.2 us
  Pallas kernels  28.6 us (96%)
  between operations  0.64 us (2%)
    pallas_call x1, Pallas kernels, fused_on_device(): pl.pallas_call(functools.partial(fused_kernel, shards, uly), out_shape=ja...  27.8 us
    pallas_call x1, Pallas kernels, fused_on_device(): pl.pallas_call(write_out, out_shape=[jax.ShapeDtypeStruct((tok, width), j...  0.77 us

profile of v3, /device:TPU:0, one launch (start us, length us, event | category | flops | bytes accessed | tf_op | source)
XLA Modules:
  0.0 29.2 jit_solution(6566932596990174739)
XLA Ops:
  0.6 27.8 %shard_map.85.held = bf16[3,64,1024]{2,1,0:T(8,128)(2,1)S(1)} custom-call(s32[3,16]{1,0:T(4,128)} %bitcast.1, bf16[64,1024]{1,0:T(8,128)(2,1)} %q_ref.1, bf16[64,1024]{1,0:T(8,128)(2,1)} %k_ref.1, bf16[64,1024]{1,0:T(8,128)(2,1)} %v_ref.1, bf16[64,1024]{1,0:T(8,128)(2,1)} %o_ref.1, bf16[64,1024]{1,0:T(8,128)(2,1)} %g_ref.1), custom_call_target="tpu_custom_call" | custom-call | tf_op jit(solution)/shard_map/pallas_call | solution.py:843
  28.4 0.8 %shard_map.86 = (bf16[64,1024]{1,0:T(8,128)(2,1)}, bf16[64,1024]{1,0:T(8,128)(2,1)}, bf16[64,1024]{1,0:T(8,128)(2,1)}) custom-call(bf16[3,64,1024]{2,1,0:T(8,128)(2,1)S(1)} %shard_map.85.held), custom_call_target="tpu_custom_call" | custom-call | tf_op jit(solution)/shard_map/pallas_call | solution.py:877

commit v4 on v3

--- a/solution.py
+++ b/solution.py
@@ -298,7 +298,7 @@
 COLS_BY_COLS = (((0,), (0,)), ((), ()))
 
 
-FIRST_TILES = ((0, 0), (1, 0), (2, 0), (3, 0), (3, 3), (3, 2), (2, 2), (1, 1), (3, 1), (2, 1))
+FIRST_TILES = ((0, 0), (1, 0), (2, 0), (3, 0), (3, 3), (3, 2), (3, 1), (2, 2), (1, 1), (2, 1))
 
 
 def flip(value, mask, count):
@@ -437,10 +437,9 @@
 
         @pl.when(is_home)
         def _():
-            for j in range(shards // 2):
-                s = 2 * j + (core + j) % 2
-                for mask in reversed(range(uly)):
-                    place = (s, flip(u, mask, uly))
+            for p in range(uly):
+                for j in range(shards // 2):
+                    place = (2 * j + (core + j) % 2, p)
                     pl.when(jnp.logical_not(is_self(place)))(functools.partial(greet, place))
             greet(sibling)
 
@@ -596,13 +595,15 @@
                     probs = scores[slot[q, k], low:high, first:] * factor[:, first:]
                     probs_low[slot[q, k], low:high, first:] = probs.astype(jnp.bfloat16)
 
-        def add(ref, value, fresh):
-            if fresh:
+        def add(ref, value, fresh, result=None):
+            if not fresh:
+                value = value + ref[...]
+            if result is None:
                 ref[...] = value
             else:
-                ref[...] += value
-
-        def make_values(q, k, start, stop, fresh):
+                result[...] = value.astype(jnp.bfloat16)
+
+        def make_values(q, k, start, stop, fresh, last):
             with jax.named_scope(f"values_{q}_{k}"):
                 for low, high, first in pieces_of(q, k, start, stop):
                     product = jnp.dot(
@@ -610,7 +611,8 @@
                         held[GRAD, q, first:, :],
                         preferred_element_type=f32,
                     )
-                    add(acc.at[D_VALUE, k, low:high, :], product, fresh)
+                    result = outgoing.at[D_VALUE, k // 2, low:high, :] if last else None
+                    add(acc.at[D_VALUE, k, low:high, :], product, fresh, result)
 
         def make_grads(q, k, factor, delta):
             with jax.named_scope(f"grads_{q}_{k}"):
@@ -628,7 +630,7 @@
                     )
                     score_grads[:count, lanes(a)] = grads.astype(jnp.bfloat16)
 
-        def add_query(q, k, a, fresh):
+        def add_query(q, k, a, fresh, last):
             count = keys_for(q, k, a)
             product = lax.dot_general(
                 score_grads[:count, lanes(a)],
@@ -636,20 +638,21 @@
                 COLS_BY_COLS,
                 preferred_element_type=f32,
             )
-            add(acc.at[D_QUERY, q, lanes(a), :], product, fresh)
-
-        def add_key(q, k, r, fresh):
+            result = outgoing.at[D_QUERY, q // 2, lanes(a), :] if last else None
+            add(acc.at[D_QUERY, q, lanes(a), :], product, fresh, result)
+
+        def add_key(q, k, r, fresh, last):
             first = first_lane(q, k, r)
             product = jnp.dot(
                 score_grads[lanes(r), first:],
                 held[QUERY, q, first:, :],
                 preferred_element_type=f32,
             )
-            add(acc.at[D_KEY, k, lanes(r), :], product, fresh)
+            result = outgoing.at[D_KEY, k // 2, lanes(r), :] if last else None
+            add(acc.at[D_KEY, k, lanes(r), :], product, fresh, result)
 
         def send_result(t, s, start=0, stop=length):
             with jax.named_scope(f"send_{t}_{s}_{start}"):
-                outgoing[t, s // 2, start:stop, :] = acc[t, s, start:stop, :].astype(jnp.bfloat16)
                 inner, outer = 2 * base, 2 * (base + planes)
                 targets = [(p, False) for p in range(uly) if not inner <= p < outer]
                 for mask in reversed(range(outer - inner)):
@@ -669,17 +672,19 @@
         own(QUERY)
         tops, totals = {}, {}
 
-        def all_scores(q):
-            for k in owned:
-                if k <= q:
-                    tops[q] = make_scores(q, k, tops.get(q))
-            totals[q] = make_exps(q, tops[q])
-
-        for q in lent + q_far:
-            if q in q_far:
-                with jax.named_scope("lent_q"):
-                    lent_copy(QUERY, q).wait_recv()
-            all_scores(q)
+        def all_scores(queries):
+            for q in queries:
+                for k in owned:
+                    if k <= q:
+                        tops[q] = make_scores(q, k, tops.get(q))
+            for q in queries:
+                totals[q] = make_exps(q, tops[q])
+
+        all_scores(lent if c else [])
+        with jax.named_scope("lent_q"):
+            for q in q_far:
+                lent_copy(QUERY, q).wait_recv()
+        all_scores(q_far if c else lent + q_far)
         with jax.named_scope("stats"):
             remote(delta_recv, delta_recv, ds_sem.at[0], dr_sem.at[0], (b, u)).wait_recv()
             for s in owned:
@@ -691,9 +696,7 @@
                     pieces.append(piece)
                 stats[c, s, 2:3, :] = jnp.concatenate(pieces, axis=1)
             remote(stats.at[c], stats.at[c], st.at[c], st.at[c], sibling).start()
-        for q in q_own:
-            if q not in lent:
-                all_scores(q)
+        all_scores([q for q in q_own if q not in lent])
         own(GRAD)
         with jax.named_scope("stats_wait"):
             remote(stats.at[1 - c], stats.at[1 - c], st.at[c], st.at[1 - c], sibling).wait_recv()
@@ -727,7 +730,7 @@
                         with jax.named_scope("lent_g"):
                             lent_copy(GRAD, q).wait_recv()
                         have.add(q)
-                    make_values(q, k, start, stop, q == queries[0])
+                    make_values(q, k, start, stop, q == queries[0], q == queries[-1])
                 send_result(D_VALUE, k, start, stop)
         own(VALUE)
         todo = [tile for tile in FIRST_TILES if tile in tiles]
@@ -740,20 +743,24 @@
                 with jax.named_scope(f"partial_{q}"):
                     ref = partial.at[q]
                     remote(ref, ref, pt.at[q], pt.at[q], sibling).wait_recv()
-                    acc[D_QUERY, q] += partial[q]
+                    total = acc[D_QUERY, q] + partial[q]
+                    outgoing[D_QUERY, q // 2] = total.astype(jnp.bfloat16)
                 send_result(D_QUERY, q)
 
         while todo:
             q, k = todo.pop(0)
             make_grads(q, k, factors[q] * scale, deltas[q])
             fresh_query, fresh_key = starts("q", q), starts("k", k)
+            last_query = all(tile[0] != q for tile in todo)
+            last_key = all(tile[1] != k for tile in todo)
+            whole_query = last_query and q in q_own and q not in lent
             with jax.named_scope(f"dots_{q}_{k}"):
                 for a in range(2):
-                    add_query(q, k, a, fresh_query)
+                    add_query(q, k, a, fresh_query, whole_query)
                 for r in range(2):
-                    add_key(q, k, r, fresh_key)
+                    add_key(q, k, r, fresh_key, last_key)
             finish_queries()
-            if all(tile[0] != q for tile in todo):
+            if last_query:
                 if q in q_far:
                     ref = acc.at[D_QUERY, q]
                     remote(ref, partial.at[q], pt.at[q], pt.at[q], sibling).start()
@@ -761,7 +768,7 @@
                     waiting.append(q)
                 else:
                     send_result(D_QUERY, q)
-            if all(tile[1] != k for tile in todo):
+            if last_key:
                 send_result(D_KEY, k)
         finish_queries()
         with jax.named_scope("lent_sent"):
@@ -816,9 +823,13 @@
 
 
 def write_out(held, a_out, b_out, c_out, done):
+    half = held.shape[1] // 2
     writes = [
-        pltpu.make_async_copy(held.at[i], target, done.at[i])
+        pltpu.make_async_copy(
+            held.at[i, pl.ds(n * half, half)], target.at[pl.ds(n * half, half)], done.at[2 * i + n]
+        )
         for i, target in enumerate((a_out, b_out, c_out))
+        for n in range(2)
     ]
     for write in writes:
         write.start()
@@ -879,7 +890,7 @@
         out_shape=[jax.ShapeDtypeStruct((tok, width), jnp.bfloat16)] * 3,
         in_specs=[vmem],
         out_specs=[hbm] * 3,
-        scratch_shapes=[dma((3,))],
+        scratch_shapes=[dma((6,))],
         compiler_params=pltpu.CompilerParams(vmem_limit_bytes=32 * 1024 * 1024),
     )(results)
 

time: 29.8 us -> 29.6 us (level)
  no operation moved by 1% of the time
where the time goes in v4:
time: 29.6 us; the launch traced here: 29.2 us
  Pallas kernels  28.5 us (96%)
  between operations  0.64 us (2%)
    pallas_call x1, Pallas kernels, fused_on_device(): pl.pallas_call(functools.partial(fused_kernel, shards, uly), out_shape=ja...  27.8 us
    pallas_call x1, Pallas kernels, fused_on_device(): pl.pallas_call(write_out, out_shape=[jax.ShapeDtypeStruct((tok, width), j...  0.79 us

profile of v4, /device:TPU:0, one launch (start us, length us, event | category | flops | bytes accessed | tf_op | source)
XLA Modules:
  0.0 29.2 jit_solution(4924894388930211649)
XLA Ops:
  0.6 27.8 %shard_map.85.held = bf16[3,64,1024]{2,1,0:T(8,128)(2,1)S(1)} custom-call(s32[3,16]{1,0:T(4,128)} %bitcast.1, bf16[64,1024]{1,0:T(8,128)(2,1)} %q_ref.1, bf16[64,1024]{1,0:T(8,128)(2,1)} %k_ref.1, bf16[64,1024]{1,0:T(8,128)(2,1)} %v_ref.1, bf16[64,1024]{1,0:T(8,128)(2,1)} %o_ref.1, bf16[64,1024]{1,0:T(8,128)(2,1)} %g_ref.1), custom_call_target="tpu_custom_call" | custom-call | tf_op jit(solution)/shard_map/pallas_call | solution.py:854
  28.4 0.8 %shard_map.86 = (bf16[64,1024]{1,0:T(8,128)(2,1)}, bf16[64,1024]{1,0:T(8,128)(2,1)}, bf16[64,1024]{1,0:T(8,128)(2,1)}) custom-call(bf16[3,64,1024]{2,1,0:T(8,128)(2,1)S(1)} %shard_map.85.held), custom_call_target="tpu_custom_call" | custom-call | tf_op jit(solution)/shard_map/pallas_call | solution.py:888

commit v5 on v4

--- a/solution.py
+++ b/solution.py
@@ -566,7 +566,7 @@
             totals = []
             with jax.named_scope(f"exps_{q}"):
                 for a in range(2):
-                    top = jnp.max(tops[a], axis=0, keepdims=True)
+                    top = jnp.maximum(jnp.max(tops[a], axis=0, keepdims=True), 0.1 * NEG)
                     total = jnp.zeros((8, wide), f32)
                     for k in owned:
                         if k > q:

time: 29.6 us -> 29.6 us (level)
  no operation moved by 1% of the time
where the time goes in v5:
time: 29.6 us; the launch traced here: 29.2 us
  Pallas kernels  28.5 us (96%)
  between operations  0.64 us (2%)
    pallas_call x1, Pallas kernels, fused_on_device(): pl.pallas_call(functools.partial(fused_kernel, shards, uly), out_shape=ja...  27.8 us
    pallas_call x1, Pallas kernels, fused_on_device(): pl.pallas_call(write_out, out_shape=[jax.ShapeDtypeStruct((tok, width), j...  0.79 us

profile of v5, /device:TPU:0, one launch (start us, length us, event | category | flops | bytes accessed | tf_op | source)
XLA Modules:
  0.0 29.2 jit_solution(1942154431919317366)
XLA Ops:
  0.6 27.8 %shard_map.85.held = bf16[3,64,1024]{2,1,0:T(8,128)(2,1)S(1)} custom-call(s32[3,16]{1,0:T(4,128)} %bitcast.1, bf16[64,1024]{1,0:T(8,128)(2,1)} %q_ref.1, bf16[64,1024]{1,0:T(8,128)(2,1)} %k_ref.1, bf16[64,1024]{1,0:T(8,128)(2,1)} %v_ref.1, bf16[64,1024]{1,0:T(8,128)(2,1)} %o_ref.1, bf16[64,1024]{1,0:T(8,128)(2,1)} %g_ref.1), custom_call_target="tpu_custom_call" | custom-call | tf_op jit(solution)/shard_map/pallas_call | solution.py:854
  28.4 0.8 %shard_map.86 = (bf16[64,1024]{1,0:T(8,128)(2,1)}, bf16[64,1024]{1,0:T(8,128)(2,1)}, bf16[64,1024]{1,0:T(8,128)(2,1)}) custom-call(bf16[3,64,1024]{2,1,0:T(8,128)(2,1)S(1)} %shard_map.85.held), custom_call_target="tpu_custom_call" | custom-call | tf_op jit(solution)/shard_map/pallas_call | solution.py:888
